TPU v7x, 32 devices: a whole 2x2x4 slice. The times are simulated.
32 devices in a mesh: shard: 2 (over core), context: 4 (over y, x), tensor: 4 (over z).
Axes of the slice: x: 2, y: 2, z: 4, core: 2. Of those that a mesh axis runs over, the one named last changes fastest.
Arguments:
- tokens: bfloat16 [2, 4096, 1536], P('shard', 'context'), may hold values from -6 to 6
- w_query: bfloat16 [1536, 1536], P('shard', 'tensor'), may hold values from -0.15625 to 0.15625
- key_weight: bfloat16 [1536, 768], P('shard', 'tensor'), may hold values from -0.15625 to 0.15625
- value_weight: bfloat16 [1536, 768], P('shard', 'tensor'), may hold values from -0.15625 to 0.15625
- w_out: bfloat16 [1536, 1536], P('tensor', 'shard'), may hold values from -0.625 to 0.625
- w_gate: bfloat16 [1536, 4096], P('shard', 'tensor'), may hold values from -0.15625 to 0.15625
- w_up: bfloat16 [1536, 4096], P('shard', 'tensor'), may hold values from -0.15625 to 0.15625
- w_down: bfloat16 [4096, 1536], P('tensor', 'shard'), may hold values from -0.09375 to 0.09375
- gain_attn: bfloat16 [1536], P('shard'), may hold values from 0.5 to 1.5
- gain_ffn: bfloat16 [1536], P('shard'), may hold values from 0.5 to 1.5
- segments: int32 [2, 4096], P('shard'), may hold values from 0 to 8, as said below
- positions: int32 [2, 4096], P('shard'), may hold values from 0 to 2303, as said below
- cotangent: bfloat16 [2, 4096, 1536], P('shard', 'context'), may hold values from -6 to 6
Outputs:
- output: bfloat16 [2, 4096, 1536], P('shard', 'context')
- tokens_grad: bfloat16 [2, 4096, 1536], P('shard', 'context')
- w_query_grad: float32 [1536, 1536], P('shard', 'tensor')
- w_key_grad: float32 [1536, 768], P('shard', 'tensor')
- w_value_grad: float32 [1536, 768], P('shard', 'tensor')
- w_out_grad: float32 [1536, 1536], P('tensor', 'shard')
- w_gate_grad: float32 [1536, 4096], P('shard', 'tensor')
- w_up_grad: float32 [1536, 4096], P('shard', 'tensor')
- w_down_grad: float32 [4096, 1536], P('tensor', 'shard')
- gain_attn_grad: float32 [1536], P('shard')
- gain_ffn_grad: float32 [1536], P('shard')
Inputs may be any that keep to these rules, and one draw needn't show every extreme that they name: In each group, segment 0 is a prompt of 2048 tokens and segments 1 to 8 are continuations of 256 tokens each; continuation number c branches off the prompt after its first c * 256 positions. Even slots 2 i hold the prompt half and odd slots 2 i + 1 the continuation half, each half being 2048 rows indexed by i. The prompt half is made of runs of 256 rows, each run holding 256 consecutive prompt tokens in order, the order of the runs drawn; the continuation half is made of runs of 256 rows, each run one whole continuation in order, the order of the continuations drawn. A prompt token's position is its index in the prompt; a continuation's token is at 2048 plus its index in the continuation; positions rise by one along each aligned block of 256 rows of a half.
All inputs are finite; a program needn't handle non-finite values.
Results may differ from a plain program's by a relative error of at most 0.015.
Values may be sent and summed in bfloat16 or wider, within the bound.
A program may use at most 384 MiB of HBM per device.

v0:
```python
import math

import jax
import jax.numpy as jnp
from jax import lax
from jax.sharding import PartitionSpec as P

HEAD_SIZE = 96
CLEN = 256


rope_base = 100000.0
norm_eps = 1e-05


def tables(positions):
    half_width = HEAD_SIZE // 2
    frequency = jnp.exp(
        jnp.arange(half_width, dtype=jnp.float32) * (-2.0 * math.log(rope_base) / HEAD_SIZE)
    )
    angles = positions.astype(jnp.float32)[:, None] * frequency[None, :]
    return (jnp.cos(angles)[:, None, :], jnp.sin(angles)[:, None, :])


def rotary_apply(heads, cosine_table, sine_values):
    half_width = HEAD_SIZE // 2
    front_half = heads[..., :half_width]
    back_half = heads[..., half_width:]
    return jnp.concatenate(
        [
            front_half * cosine_table - back_half * sine_values,
            back_half * cosine_table + front_half * sine_values,
        ],
        axis=-1,
    )


def rotate_back(heads, cosine_table, sine_values):
    half_width = HEAD_SIZE // 2
    front_half = heads[..., :half_width]
    back_half = heads[..., half_width:]
    return jnp.concatenate(
        [
            front_half * cosine_table + back_half * sine_values,
            back_half * cosine_table - front_half * sine_values,
        ],
        axis=-1,
    )


def contract_rows(left, right):
    return lax.dot_general(
        left, right, (((0,), (0,)), ((), ())), preferred_element_type=jnp.float32
    )


def contract_cols(left, right):
    return lax.dot_general(
        left, right, (((1,), (1,)), ((), ())), preferred_element_type=jnp.float32
    )


def norm_back(tok_rows, norm_scale, gain, grad_normed):
    weighted = gain * grad_normed
    inner = jnp.mean(weighted * tok_rows, axis=-1, keepdims=True)
    grad_rows = norm_scale * weighted - tok_rows * (norm_scale * norm_scale * norm_scale) * inner
    grad_gain = jnp.sum(grad_normed * tok_rows * norm_scale, axis=0)
    return (grad_rows, grad_gain)


def visible(seg_query, pos_query, seg_keys, pos_keys):
    own = (seg_keys[None, :] == seg_query[:, None]) & (pos_keys[None, :] <= pos_query[:, None])
    branch = (
        (seg_keys[None, :] == 0)
        & (seg_query[:, None] > 0)
        & (pos_keys[None, :] < seg_query[:, None] * CLEN)
    )
    return own | branch


def body(
    tokens,
    w_query,
    key_weight,
    value_weight,
    w_out,
    w_gate,
    w_up,
    w_down,
    gain_attn,
    gain_ffn,
    segments,
    positions,
    cotangent,
):
    groups, tok_local, model_width = tokens.shape
    token_count = groups * tok_local
    heads_here = w_query.shape[1] // HEAD_SIZE
    kv_here = key_weight.shape[1] // HEAD_SIZE
    per_kv = heads_here // kv_here
    kv_width = kv_here * HEAD_SIZE
    score_scale = 1.0 / math.sqrt(HEAD_SIZE)
    context_index = lax.axis_index("context")
    first_row = context_index * tok_local
    seg_here = lax.dynamic_slice_in_dim(segments, first_row, tok_local, 1)
    pos_here = lax.dynamic_slice_in_dim(positions, first_row, tok_local, 1)
    w_query, key_weight, value_weight, w_gate, w_up, gain_attn, gain_ffn = (
        lax.all_gather(w_query, "shard", axis=0, tiled=True),
        lax.all_gather(key_weight, "shard", axis=0, tiled=True),
        lax.all_gather(value_weight, "shard", axis=0, tiled=True),
        lax.all_gather(w_gate, "shard", axis=0, tiled=True),
        lax.all_gather(w_up, "shard", axis=0, tiled=True),
        lax.all_gather(gain_attn, "shard", axis=0, tiled=True),
        lax.all_gather(gain_ffn, "shard", axis=0, tiled=True),
    )
    w_out, w_down = (
        lax.all_gather(w_out, "shard", axis=1, tiled=True),
        lax.all_gather(w_down, "shard", axis=1, tiled=True),
    )
    gain_one = gain_attn.astype(jnp.float32)
    gain_two = gain_ffn.astype(jnp.float32)
    tok_rows = tokens.reshape(token_count, model_width).astype(jnp.float32)
    scale_one = lax.rsqrt(jnp.mean(tok_rows * tok_rows, axis=-1, keepdims=True) + norm_eps)
    normed_input = (tok_rows * scale_one * gain_one).astype(jnp.bfloat16)
    cosine_table, sine_values = tables(pos_here.reshape(token_count))
    query_heads_rows = rotary_apply(
        jnp.dot(normed_input, w_query, preferred_element_type=jnp.float32).reshape(
            token_count, heads_here, HEAD_SIZE
        ),
        cosine_table,
        sine_values,
    )
    query_heads_rows = query_heads_rows.astype(jnp.bfloat16).reshape(
        groups, tok_local, heads_here * HEAD_SIZE
    )
    key_rows = rotary_apply(
        jnp.dot(normed_input, key_weight, preferred_element_type=jnp.float32).reshape(
            token_count, kv_here, HEAD_SIZE
        ),
        cosine_table,
        sine_values,
    )
    key_rows = key_rows.astype(jnp.bfloat16).reshape(token_count, kv_width)
    value_rows = jnp.dot(normed_input, value_weight, preferred_element_type=jnp.float32).astype(
        jnp.bfloat16
    )
    keyval = jnp.concatenate([key_rows, value_rows], axis=-1).reshape(
        groups, tok_local, 2 * kv_width
    )
    gathered = lax.all_gather(keyval, "context", axis=1, tiled=True)

    def scores_of(group_queries, group_keyval, seg_query, pos_query, seg_keys, pos_keys):
        grouped_heads = group_queries.reshape(tok_local, kv_here, per_kv, HEAD_SIZE)
        key_head_rows = group_keyval[:, :kv_width].reshape(-1, kv_here, HEAD_SIZE)
        scores = (
            jnp.einsum(
                "bhgd,khd->hgbk", grouped_heads, key_head_rows, preferred_element_type=jnp.float32
            )
            * score_scale
        )
        allowed = visible(seg_query, pos_query, seg_keys, pos_keys)
        return (jnp.where(allowed[None, None], scores, -1e30), grouped_heads, key_head_rows)

    def attend_group(inputs):
        group_queries, group_keyval, seg_query, pos_query, seg_keys, pos_keys = inputs
        scores, grouped_heads, key_head_rows = scores_of(
            group_queries, group_keyval, seg_query, pos_query, seg_keys, pos_keys
        )
        top_score = jnp.max(scores, axis=-1, keepdims=True)
        exponent = jnp.exp(scores - top_score)
        totals = jnp.sum(exponent, axis=-1, keepdims=True)
        soft_weights = (exponent / totals).astype(jnp.bfloat16)
        value_head_rows = group_keyval[:, kv_width:].reshape(-1, kv_here, HEAD_SIZE)
        attended_output = jnp.einsum(
            "hgbk,khd->bhgd", soft_weights, value_head_rows, preferred_element_type=jnp.float32
        )
        return (
            attended_output.reshape(tok_local, heads_here * HEAD_SIZE),
            (top_score + jnp.log(totals))[..., 0],
        )

    attended_output, log_total = lax.map(
        attend_group, (query_heads_rows, gathered, seg_here, pos_here, segments, positions)
    )
    attended_low = attended_output.reshape(token_count, heads_here * HEAD_SIZE).astype(jnp.bfloat16)
    attn_sum = lax.psum(jnp.dot(attended_low, w_out, preferred_element_type=jnp.float32), "tensor")
    middle = tok_rows + attn_sum
    scale_two = lax.rsqrt(jnp.mean(middle * middle, axis=-1, keepdims=True) + norm_eps)
    normed_two = (middle * scale_two * gain_two).astype(jnp.bfloat16)
    gate_proj = jnp.dot(normed_two, w_gate, preferred_element_type=jnp.float32)
    up_proj = jnp.dot(normed_two, w_up, preferred_element_type=jnp.float32)
    sigmoid_gate = jax.nn.sigmoid(gate_proj)
    silu_gate = gate_proj * sigmoid_gate
    hidden = (silu_gate * up_proj).astype(jnp.bfloat16)
    ffn_sum = lax.psum(
        jnp.dot(hidden, w_down, preferred_element_type=jnp.float32).astype(jnp.bfloat16), "tensor"
    ).astype(jnp.float32)
    output = (middle + ffn_sum).astype(jnp.bfloat16).reshape(groups, tok_local, model_width)
    grad_low = cotangent.reshape(token_count, model_width)
    grad_out = grad_low.astype(jnp.float32)
    grad_hidden = contract_cols(grad_low, w_down)
    grad_w_down_t = contract_rows(grad_low, hidden)
    grad_gate = (
        grad_hidden * up_proj * sigmoid_gate * (1.0 + gate_proj * (1.0 - sigmoid_gate))
    ).astype(jnp.bfloat16)
    grad_up = (grad_hidden * silu_gate).astype(jnp.bfloat16)
    grad_w_gate = contract_rows(normed_two, grad_gate)
    grad_w_up = contract_rows(normed_two, grad_up)
    grad_normed_two = lax.psum(
        contract_cols(grad_gate, w_gate) + contract_cols(grad_up, w_up), "tensor"
    )
    back_two, grad_gain_two = norm_back(middle, scale_two, gain_two, grad_normed_two)
    grad_middle = grad_out + back_two
    grad_mid_low = grad_middle.astype(jnp.bfloat16)
    grad_w_out_t = contract_rows(grad_mid_low, attended_low)
    grad_attended = (
        contract_cols(grad_mid_low, w_out)
        .astype(jnp.bfloat16)
        .reshape(groups, tok_local, heads_here * HEAD_SIZE)
    )

    def attend_back(inputs):
        (
            group_queries,
            group_keyval,
            group_grad,
            group_total,
            seg_query,
            pos_query,
            seg_keys,
            pos_keys,
        ) = inputs
        scores, grouped_heads, key_head_rows = scores_of(
            group_queries, group_keyval, seg_query, pos_query, seg_keys, pos_keys
        )
        soft_weights = jnp.exp(scores - group_total[..., None])
        value_head_rows = group_keyval[:, kv_width:].reshape(-1, kv_here, HEAD_SIZE)
        grad_grouped = group_grad.reshape(tok_local, kv_here, per_kv, HEAD_SIZE)
        grad_weights = jnp.einsum(
            "bhgd,khd->hgbk", grad_grouped, value_head_rows, preferred_element_type=jnp.float32
        )
        inner = jnp.sum(soft_weights * grad_weights, axis=-1, keepdims=True)
        grad_scores = (soft_weights * (grad_weights - inner)).astype(jnp.bfloat16)
        grad_queries = (
            jnp.einsum(
                "hgbk,khd->bhgd", grad_scores, key_head_rows, preferred_element_type=jnp.float32
            )
            * score_scale
        )
        grad_keys = (
            jnp.einsum(
                "hgbk,bhgd->khd", grad_scores, grouped_heads, preferred_element_type=jnp.float32
            )
            * score_scale
        )
        grad_values = jnp.einsum(
            "hgbk,bhgd->khd",
            soft_weights.astype(jnp.bfloat16),
            grad_grouped,
            preferred_element_type=jnp.float32,
        )
        grad_keyval = jnp.concatenate(
            [grad_keys.reshape(-1, kv_width), grad_values.reshape(-1, kv_width)], axis=-1
        )
        return (grad_queries.reshape(tok_local, heads_here * HEAD_SIZE), grad_keyval)

    grad_queries, grad_keyval = lax.map(
        attend_back,
        (
            query_heads_rows,
            gathered,
            grad_attended,
            log_total,
            seg_here,
            pos_here,
            segments,
            positions,
        ),
    )
    grad_keyval = lax.psum_scatter(grad_keyval, "context", scatter_dimension=1, tiled=True)
    grad_query_rows = rotate_back(
        grad_queries.reshape(token_count, heads_here, HEAD_SIZE), cosine_table, sine_values
    )
    grad_query_rows = grad_query_rows.astype(jnp.bfloat16).reshape(
        token_count, heads_here * HEAD_SIZE
    )
    grad_key_rows = rotate_back(
        grad_keyval[..., :kv_width].reshape(token_count, kv_here, HEAD_SIZE),
        cosine_table,
        sine_values,
    )
    grad_key_rows = grad_key_rows.astype(jnp.bfloat16).reshape(token_count, kv_width)
    grad_value_rows = (
        grad_keyval[..., kv_width:].reshape(token_count, kv_width).astype(jnp.bfloat16)
    )
    grad_w_query = contract_rows(normed_input, grad_query_rows)
    grad_w_key = contract_rows(normed_input, grad_key_rows)
    grad_w_value = contract_rows(normed_input, grad_value_rows)
    partial_one = (
        contract_cols(grad_query_rows, w_query)
        + contract_cols(grad_key_rows, key_weight)
        + contract_cols(grad_value_rows, value_weight)
    )
    grad_normed = lax.psum(partial_one, "tensor")
    back_one, grad_gain_one = norm_back(tok_rows, scale_one, gain_one, grad_normed)
    tokens_grad = (
        (grad_middle + back_one).astype(jnp.bfloat16).reshape(groups, tok_local, model_width)
    )
    summed = (
        lax.psum_scatter(grad_w_query, ("shard", "context"), scatter_dimension=0, tiled=True),
        lax.psum_scatter(grad_w_key, ("shard", "context"), scatter_dimension=0, tiled=True),
        lax.psum_scatter(grad_w_value, ("shard", "context"), scatter_dimension=0, tiled=True),
        lax.psum_scatter(grad_w_out_t, ("shard", "context"), scatter_dimension=0, tiled=True),
        lax.psum_scatter(grad_w_gate, ("shard", "context"), scatter_dimension=0, tiled=True),
        lax.psum_scatter(grad_w_up, ("shard", "context"), scatter_dimension=0, tiled=True),
        lax.psum_scatter(grad_w_down_t, ("shard", "context"), scatter_dimension=0, tiled=True),
        lax.psum_scatter(grad_gain_one, ("shard", "context"), scatter_dimension=0, tiled=True),
        lax.psum_scatter(grad_gain_two, ("shard", "context"), scatter_dimension=0, tiled=True),
    )
    summed = (
        lax.all_gather(summed[0].astype(jnp.bfloat16), "context", axis=0, tiled=True).astype(
            jnp.float32
        ),
        lax.all_gather(summed[1].astype(jnp.bfloat16), "context", axis=0, tiled=True).astype(
            jnp.float32
        ),
        lax.all_gather(summed[2].astype(jnp.bfloat16), "context", axis=0, tiled=True).astype(
            jnp.float32
        ),
        lax.all_gather(summed[3].astype(jnp.bfloat16), "context", axis=0, tiled=True).astype(
            jnp.float32
        ),
        lax.all_gather(summed[4].astype(jnp.bfloat16), "context", axis=0, tiled=True).astype(
            jnp.float32
        ),
        lax.all_gather(summed[5].astype(jnp.bfloat16), "context", axis=0, tiled=True).astype(
            jnp.float32
        ),
        lax.all_gather(summed[6].astype(jnp.bfloat16), "context", axis=0, tiled=True).astype(
            jnp.float32
        ),
        lax.all_gather(summed[7].astype(jnp.bfloat16), "context", axis=0, tiled=True).astype(
            jnp.float32
        ),
        lax.all_gather(summed[8].astype(jnp.bfloat16), "context", axis=0, tiled=True).astype(
            jnp.float32
        ),
    )
    return (
        output,
        tokens_grad,
        summed[0],
        summed[1],
        summed[2],
        summed[3].T,
        summed[4],
        summed[5],
        summed[6].T,
        summed[7],
        summed[8],
    )


def solution(mesh):
    in_specs = (
        P("shard", "context", None),
        P("shard", "tensor"),
        P("shard", "tensor"),
        P("shard", "tensor"),
        P("tensor", "shard"),
        P("shard", "tensor"),
        P("shard", "tensor"),
        P("tensor", "shard"),
        P("shard"),
        P("shard"),
        P("shard", None),
        P("shard", None),
        P("shard", "context", None),
    )
    out_specs = (
        P("shard", "context", None),
        P("shard", "context", None),
        P("shard", "tensor"),
        P("shard", "tensor"),
        P("shard", "tensor"),
        P("tensor", "shard"),
        P("shard", "tensor"),
        P("shard", "tensor"),
        P("tensor", "shard"),
        P("shard"),
        P("shard"),
    )
    return jax.shard_map(body, mesh=mesh, in_specs=in_specs, out_specs=out_specs, check_vma=False)
```

profile of v0, /device:TPU:1, one launch (start us, length us, event | category | flops | bytes accessed | tf_op | source)
XLA Modules:
  0.0 1609.2 jit_solution(5250611638059774640)
XLA Ops:
  31.4 9.5 and_or_fusion
  47.3 27.3 %all-gather.29.cloned.1.call-done = bf16[4096,384]{0,1:T(8,128)(2,1)} async-done(((bf16[1024,384]{0,1:T(8,128)(2,1)}), bf16[4096,384]{0,1:T(8,128)(2,1)}) %all-gather.29.cloned.1.call-update) | async-done | bytes 3145744 | tf_op jit(solution)/shard_map/all_gather | solution.py:150
  78.6 27.7 %fusion.71 = (f32[2,2,1024]{2,1,0:T(2,128)S(1)}, f32[2,2,1024,4096]{2,3,1,0:T(8,128)}) fusion(bf16[4096,2,96,1]{0,2,3,1:T(8,128)(2,1)} %bitcast.177, bf16[1024,2,2,48]{0,3,2,1:T(8,128)(2,1)} %bitcast.194, bf16[1024,2,2,48]{0,3,2,1:T(8,128)(2,1)S(1)} %bitcast.192, pred[1024,4096]{0,1:T(8,128)(4,1)} %and_or_fusion), kind=kOutput, calls=%fused_computation.118 | convolution fusion | flops 3273125888 | bytes 73678848 | tf_op jit(solution)/shard_map/while/body/eval_jaxpr/bhgd,khd->hgbk/dot_general | solution.py:156
  106.3 21.2 %fusion.3 = f32[2,2,1024]{2,1,0:T(2,128)S(1)} fusion(f32[2,2,1024,4096]{2,3,1,0:T(8,128)} %get-tuple-element.136, f32[2,2,1024]{2,1,0:T(2,128)S(1)} %get-tuple-element.135), kind=kLoop, calls=%fused_computation.9 | loop fusion | flops 33550336 | bytes 67141632 | tf_op jit(solution)/shard_map/while/body/eval_jaxpr/reduce_sum | solution.py:171
  127.6 24.7 %fusion.55 = bf16[2,96,2,1024]{3,1,2,0:T(8,128)(2,1)} fusion(bf16[4096,2,96,1]{0,2,3,1:T(8,128)(2,1)} %bitcast.181, f32[2,2,1024,4096]{2,3,1,0:T(8,128)} %get-tuple-element.136, f32[2,2,1024]{2,1,0:T(2,128)S(1)} %fusion.3, f32[2,2,1024]{2,1,0:T(2,128)S(1)} %get-tuple-element.135), kind=kOutput, calls=%fused_computation.79 | convolution fusion | flops 3271950336 | bytes 69500928 | tf_op jit(solution)/shard_map/while/body/eval_jaxpr/hgbk,khd->bhgd/dot_general | solution.py:174
  162.7 218.7 %all-reduce.11.cloned.1.call-done = f32[1024,1536]{1,0:T(8,128)} async-done(((f32[1024,1536]{1,0:T(8,128)}), f32[1024,1536]{1,0:T(8,128)}) %all-reduce.11.cloned.1.call-update) | async-done | bytes 6291472 | tf_op jit(solution)/shard_map/psum | solution.py:186
  424.0 9.3 multiply_convert_fusion.1
  482.6 183.3 %all-reduce.15.cloned.1.call-done = f32[1024,1536]{1,0:T(8,128)} async-done(((f32[1024,1536]{1,0:T(8,128)}), f32[1024,1536]{1,0:T(8,128)}) %all-reduce.15.cloned.1.call-update) | async-done | bytes 6291472 | tf_op jit(solution)/shard_map/psum | solution.py:209
  672.5 116.4 %all-reduce.13.cloned.1.call-done = bf16[1024,1536]{1,0:T(8,128)(2,1)} async-done(((bf16[1024,1536]{1,0:T(8,128)(2,1)}), bf16[1024,1536]{1,0:T(8,128)(2,1)}) %all-reduce.13.cloned.1.call-update) | async-done | bytes 3145744 | tf_op jit(solution)/shard_map/psum | solution.py:195
  800.4 45.7 %fusion = (f32[2,2,1024]{2,1,0:T(2,128)S(1)}, f32[2,4096,1024,2]{2,1,3,0:T(8,128)}) fusion(f32[2,2,1024,4096]{2,3,1,0:T(8,128)} %get-tuple-element.136, f32[2,2,1024]{2,1,0:T(2,128)S(1)} %log_add_fusion, bf16[4096,2,96,1]{0,2,3,1:T(8,128)(2,1)S(1)} %bitcast.182, bf16[1024,2,2,96]{0,3,2,1:T(8,128)(2,1)S(1)} %bitcast.179), kind=kOutput, calls=%fused_computation.2 | convolution fusion | flops 3271553024 | bytes 136609792 | tf_op jit(solution)/shard_map/while/body/eval_jaxpr/bhgd,khd->hgbk/dot_general | solution.py:239
  846.1 57.7 %fusion.2 = bf16[2,2,1024,4096]{2,3,1,0:T(8,128)(2,1)} fusion(f32[2,4096,1024,2]{2,1,3,0:T(8,128)} %get-tuple-element.138, f32[2,2,1024,4096]{2,3,1,0:T(8,128)} %get-tuple-element.136, f32[2,2,1024]{2,1,0:T(2,128)S(1)} %get-tuple-element.137, f32[2,2,1024]{2,1,0:T(2,128)S(1)} %log_add_fusion), kind=kLoop, calls=%fused_computation.4 | loop fusion | flops 67108864 | bytes 167804928 | tf_op jit(solution)/shard_map/while/body/eval_jaxpr/convert_element_type | solution.py:243
  903.8 16.3 %fusion.27 = f32[2,96,4096]{2,1,0:T(8,128)S(1)} fusion(bf16[2,2,1024,4096]{2,3,1,0:T(8,128)(2,1)} %fusion.2, bf16[1024,2,2,48]{0,3,2,1:T(8,128)(2,1)} %bitcast.195, bf16[1024,2,2,48]{0,3,2,1:T(8,128)(2,1)S(1)} %bitcast.193), kind=kOutput, calls=%fused_computation.44 | convolution fusion | flops 3223584768 | bytes 37486592 | tf_op jit(solution)/shard_map/while/body/eval_jaxpr/hgbk,bhgd->khd/dot_general | solution.py:251
  920.1 28.2 %fusion.5 = f32[2,96,4096,1]{2,1,3,0:T(8,128)} fusion(bf16[1024,2,2,96]{0,3,2,1:T(8,128)(2,1)} %bitcast.180, f32[2,2,1024,4096]{2,3,1,0:T(8,128)} %get-tuple-element.136, f32[2,2,1024]{2,1,0:T(2,128)S(1)} %log_add_fusion), kind=kOutput, calls=%fused_computation.11 | convolution fusion | flops 3254779904 | bytes 71057408 | tf_op jit(solution)/shard_map/while/body/eval_jaxpr/hgbk,bhgd->khd/dot_general | solution.py:256
  954.9 13.6 convolution_multiply_fusion
  986.8 69.4 %reduce-scatter.11.cloned.1.call-done = f32[1,1024,384]{1,2,0:T(8,128)} async-done(((f32[1,4096,384]{1,2,0:T(8,128)}), f32[1,1024,384]{1,2,0:T(8,128)}) %reduce-scatter.11.cloned.1.call-update) | async-done | bytes 1572880 | tf_op jit(solution)/shard_map/reduce_scatter | solution.py:280
  1076.0 26.4 %reduce-scatter.13.cloned.1.call-done = f32[192,384]{1,0:T(8,128)} async-done(((f32[1536,384]{1,0:T(8,128)}), f32[192,384]{1,0:T(8,128)}) %reduce-scatter.13.cloned.1.call-update) | async-done | bytes 294928 | tf_op jit(solution)/shard_map/reduce_scatter | solution.py:310
  1112.7 35.9 %reduce-scatter.19.cloned.1.call-done = f32[192,384]{1,0:T(8,128)} async-done(((f32[1536,384]{1,0:T(8,128)}), f32[192,384]{1,0:T(8,128)}) %reduce-scatter.19.cloned.1.call-update) | async-done | bytes 294928 | tf_op jit(solution)/shard_map/reduce_scatter | solution.py:313
  1161.5 20.1 %all-gather.27.cloned.1.call-done = bf16[768,1024]{1,0:T(8,128)(2,1)} async-done(((bf16[192,1024]{1,0:T(8,128)(2,1)}), bf16[768,1024]{1,0:T(8,128)(2,1)}) %all-gather.27.cloned.1.call-update) | async-done | bytes 1572880 | tf_op jit(solution)/shard_map/all_gather | solution.py:339
  1188.7 26.1 %all-gather.23.cloned.1.call-done = bf16[768,1024]{1,0:T(8,128)(2,1)} async-done(((bf16[192,1024]{1,0:T(8,128)(2,1)}), bf16[768,1024]{1,0:T(8,128)(2,1)}) %all-gather.23.cloned.1.call-update) | async-done | bytes 1572880 | tf_op jit(solution)/shard_map/all_gather | solution.py:333
  1218.3 29.1 %all-gather.25.cloned.1.call-done = bf16[768,1024]{1,0:T(8,128)(2,1)} async-done(((bf16[192,1024]{1,0:T(8,128)(2,1)}), bf16[768,1024]{1,0:T(8,128)(2,1)}) %all-gather.25.cloned.1.call-update) | async-done | bytes 1572880 | tf_op jit(solution)/shard_map/all_gather | solution.py:336
  1250.8 38.7 %reduce-scatter.15.cloned.1.call-done = f32[192,192]{1,0:T(8,128)} async-done(((f32[1536,192]{1,0:T(8,128)}), f32[192,192]{1,0:T(8,128)}) %reduce-scatter.15.cloned.1.call-update) | async-done | bytes 147472 | tf_op jit(solution)/shard_map/reduce_scatter | solution.py:311
  1298.9 32.2 %reduce-scatter.17.cloned.1.call-done = f32[192,192]{1,0:T(8,128)} async-done(((f32[1536,192]{1,0:T(8,128)}), f32[192,192]{1,0:T(8,128)}) %reduce-scatter.17.cloned.1.call-update) | async-done | bytes 147472 | tf_op jit(solution)/shard_map/reduce_scatter | solution.py:312
  1340.4 216.0 %all-reduce.17.cloned.1.call-done = f32[1024,1536]{1,0:T(8,128)} async-done(((f32[1024,1536]{1,0:T(8,128)}), f32[1024,1536]{1,0:T(8,128)}) %all-reduce.17.cloned.1.call-update) | async-done | bytes 6291472 | tf_op jit(solution)/shard_map/psum | solution.py:304
  1560.6 27.4 %all-reduce.4 = (bf16[1536]{0:T(1024)(128)(2,1)S(1)}, bf16[1536]{0:T(1024)(128)(2,1)S(1)}) all-reduce(f32[1536]{0:T(1024)S(1)} %get-tuple-element.106, f32[1536]{0:T(1024)S(1)} %copy-done.30), channel_id=11, replica_groups=mesh['shard'=2,'context'=4,'tensor'=4] {'shard','context'}, use_global_device_ids=true, to_apply=%region_20.21.clone | all-reduce | flops 3072 | bytes 18432
  (223 shorter events, 271.9 us)
Async XLA Ops:
  7.2 33.7 %all-gather.13.cloned.1.call-start = ((), (), s32[]{:S(2)}) async-start(), calls=%async_computation.8 | async-start | bytes 1769472 | tf_op jit(solution)/shard_map/all_gather | solution.py:108
  7.9 66.7 %all-gather.29.cloned.1.call-start = ((), (), s32[]{:S(2)}) async-start(), calls=%async_computation.27 | async-start | bytes 3932160 | tf_op jit(solution)/shard_map/all_gather | solution.py:150
  28.7 123.6 %all-gather.15.cloned.1.call-start = ((), (), s32[]{:S(2)}) async-start(), calls=%async_computation.9 | async-start | bytes 1769472 | tf_op jit(solution)/shard_map/all_gather | solution.py:117
  29.4 352.0 %all-reduce.11.cloned.1.call-start = ((), (), s32[]{:S(2)}) async-start(), calls=%async_computation.10 | async-start | bytes 12582912 | tf_op jit(solution)/shard_map/psum | solution.py:186
  158.3 236.0 %all-gather.17.cloned.1.call-start = ((), (), s32[]{:S(2)}) async-start(), calls=%async_computation.11 | async-start | bytes 4718592 | tf_op jit(solution)/shard_map/all_gather | solution.py:111
  158.9 250.2 %all-gather.19.cloned.1.call-start = ((), (), s32[]{:S(2)}) async-start(), calls=%async_computation.12 | async-start | bytes 4718592 | tf_op jit(solution)/shard_map/all_gather | solution.py:112
  159.5 264.5 %all-gather.21.cloned.1.call-start = ((), (), s32[]{:S(2)}) async-start(), calls=%async_computation.13 | async-start | bytes 4718592 | tf_op jit(solution)/shard_map/all_gather | solution.py:118
  160.3 505.7 %all-reduce.15.cloned.1.call-start = ((), (), s32[]{:S(2)}) async-start(), calls=%async_computation.15 | async-start | bytes 12582912 | tf_op jit(solution)/shard_map/psum | solution.py:209
  442.3 346.6 %all-reduce.13.cloned.1.call-start = ((), (), s32[]{:S(2)}) async-start(), calls=%async_computation.14 | async-start | bytes 6291456 | tf_op jit(solution)/shard_map/psum | solution.py:195
  450.4 530.3 %reduce-scatter.25.cloned.1.call-start = ((), (), s32[]{:S(2)}) async-start(), calls=%async_computation.28 | async-start | bytes 7077888 | tf_op jit(solution)/shard_map/reduce_scatter | solution.py:316
  464.5 518.2 %reduce-scatter.21.cloned.1.call-start = ((), (), s32[]{:S(2)}) async-start(), calls=%async_computation.22 | async-start | bytes 7077888 | tf_op jit(solution)/shard_map/reduce_scatter | solution.py:314
  473.2 511.6 %reduce-scatter.23.cloned.1.call-start = ((), (), s32[]{:S(2)}) async-start(), calls=%async_computation.24 | async-start | bytes 7077888 | tf_op jit(solution)/shard_map/reduce_scatter | solution.py:315
  482.5 573.7 %reduce-scatter.11.cloned.1.call-start = ((), (), s32[]{:S(2)}) async-start(), calls=%async_computation.16 | async-start | bytes 7864320 | tf_op jit(solution)/shard_map/reduce_scatter | solution.py:280
  846.1 57.7 %copy-start.18 = (bf16[1024,4,48]{0,2,1:T(8,128)(2,1)S(1)}, bf16[1024,4,48]{0,2,1:T(8,128)(2,1)}, u32[]{:S(2)}) copy-start(bf16[1024,4,48]{0,2,1:T(8,128)(2,1)} %get-tuple-element.123) | copy-start | bytes 1179652
  953.5 148.8 %reduce-scatter.13.cloned.1.call-start = ((), (), s32[]{:S(2)}) async-start(), calls=%async_computation.18 | async-start | bytes 2654208 | tf_op jit(solution)/shard_map/reduce_scatter | solution.py:310
  974.3 174.3 %reduce-scatter.19.cloned.1.call-start = ((), (), s32[]{:S(2)}) async-start(), calls=%async_computation.21 | async-start | bytes 2654208 | tf_op jit(solution)/shard_map/reduce_scatter | solution.py:313
  980.6 201.1 %all-gather.27.cloned.1.call-start = ((), (), s32[]{:S(2)}) async-start(), calls=%async_computation.26 | async-start | bytes 1966080 | tf_op jit(solution)/shard_map/all_gather | solution.py:339
  982.6 232.2 %all-gather.23.cloned.1.call-start = ((), (), s32[]{:S(2)}) async-start(), calls=%async_computation.23 | async-start | bytes 1966080 | tf_op jit(solution)/shard_map/all_gather | solution.py:333
  984.7 262.7 %all-gather.25.cloned.1.call-start = ((), (), s32[]{:S(2)}) async-start(), calls=%async_computation.25 | async-start | bytes 1966080 | tf_op jit(solution)/shard_map/all_gather | solution.py:336
  986.7 302.8 %reduce-scatter.15.cloned.1.call-start = ((), (), s32[]{:S(2)}) async-start(), calls=%async_computation.19 | async-start | bytes 1769472 | tf_op jit(solution)/shard_map/reduce_scatter | solution.py:311
  1060.0 271.0 %reduce-scatter.17.cloned.1.call-start = ((), (), s32[]{:S(2)}) async-start(), calls=%async_computation.20 | async-start | bytes 1769472 | tf_op jit(solution)/shard_map/reduce_scatter | solution.py:312
  1063.7 492.7 %all-reduce.17.cloned.1.call-start = ((), (), s32[]{:S(2)}) async-start(), calls=%async_computation.17 | async-start | bytes 12582912 | tf_op jit(solution)/shard_map/psum | solution.py:304
  1340.4 220.2 %copy-start.30 = (f32[1536]{0:T(1024)S(1)}, f32[1536]{0:T(1024)}, u32[]{:S(2)}) copy-start(f32[1536]{0:T(1024)} %get-tuple-element.104) | copy-start | bytes 18436
  1340.4 255.1 %copy-start.31 = (f32[1024]{0:T(1024)S(1)}, f32[1024]{0:T(1024)}, u32[]{:S(2)}) copy-start(f32[1024]{0:T(1024)} %get-tuple-element.131) | copy-start | bytes 12292
  (37 other events, 306.4 us)
Sparse Core Ops, SparseCore 0:
  9.5 11.6 all-gather.12
  28.8 45.7 all-gather.28
  76.1 9.7 all-gather.14
  158.5 222.8 all-reduce.10
  382.8 11.5 all-gather.16
  395.8 13.2 all-gather.18
  410.6 13.2 all-gather.20
  442.4 223.4 all-reduce.14
  668.9 119.9 all-reduce.12
  792.1 60.7 reduce-scatter.24
  856.3 61.7 reduce-scatter.20
  921.3 61.8 reduce-scatter.22
  986.1 70.0 reduce-scatter.10
  1060.0 42.3 reduce-scatter.12
  1106.1 42.3 reduce-scatter.18
  1150.8 30.8 all-gather.26
  1183.9 30.8 all-gather.22
  1216.5 30.8 all-gather.24
  1251.2 38.2 reduce-scatter.14
  1292.7 38.3 reduce-scatter.16
  1333.4 222.9 all-reduce.16
where the time goes:
time: 1620 us; the launch traced here: 1610 us
  waiting for transfers between devices  1060 us (65%)
  matrix products  261 us (16%)
  other arithmetic  156 us (10%)
  blocking collectives  74.8 us (5%)
  local copies, waits for them, and re-layouts  36.4 us (2%)
  between operations  16.5 us (1%)
    psum x1, waiting for transfers between devices, body(): lax.psum(jnp.dot(attended_low, w_out, preferred_element_type=jnp.float32)...  219 us
    psum x1, waiting for transfers between devices, body(): grad_normed = lax.psum(partial_one, 'tensor')  216 us
    psum x1, waiting for transfers between devices, body(): lax.psum(contract_cols(grad_gate, w_gate) + contract_cols(grad_up, w_up),...  183 us
    psum x1, waiting for transfers between devices, body(): lax.psum(jnp.dot(hidden, w_down, preferred_element_type=jnp.float32).asty...  116 us
    reduce_scatter x1, waiting for transfers between devices, body(): lax.psum_scatter(grad_keyval, 'context', scatter_dimension=1, tiled=True)  69.4 us
    convert_element_type x1, other arithmetic, attend_back(): grad_scores = (soft_weights * (grad_weights - inner)).astype(jnp.bfloat16)  57.7 us
    dot_general x1, matrix products, attend_back(): jnp.einsum('bhgd,khd->hgbk', grad_grouped, value_head_rows, preferred_ele...  45.7 us
    dot_general x7, matrix products, contract_rows(): lax.dot_general(left, right, (((0,), (0,)), ((), ())), preferred_element_...  40.4 us
  transfers between devices with their start and end apart: 21, of which 16 were waited for; matrix products, arithmetic and copies ran while one was open for 25% of the time, Pallas kernels for 0%

commit v1 on v0

--- a/solution.py
+++ b/solution.py
@@ -1,8 +1,12 @@
+import functools
 import math
 
 import jax
 import jax.numpy as jnp
+import numpy as np
 from jax import lax
+from jax.experimental import pallas as pl
+from jax.experimental.pallas import tpu as pltpu
 from jax.sharding import PartitionSpec as P
 
 HEAD_SIZE = 96
@@ -78,7 +82,7 @@
     return own | branch
 
 
-def body(
+def general(
     tokens,
     w_query,
     key_weight,
@@ -361,6 +365,842 @@
     )
 
 
+MESH = pl.DeviceIdType.MESH
+RUN = 256
+PAD = 128
+NEG = -1e30
+LOG2E = 1.4426950408889634
+BF = jnp.bfloat16
+F32 = jnp.float32
+VLIM = 64 * 1024 * 1024
+
+
+def mm(a, b):
+    return lax.dot_general(a, b, (((1,), (0,)), ((), ())), preferred_element_type=F32)
+
+
+def mm_nt(a, b):
+    return lax.dot_general(a, b, (((1,), (1,)), ((), ())), preferred_element_type=F32)
+
+
+def mm_tn(a, b):
+    return lax.dot_general(a, b, (((0,), (0,)), ((), ())), preferred_element_type=F32)
+
+
+def iota(shape, axis):
+    return lax.broadcasted_iota(jnp.int32, shape, axis)
+
+
+def one_hot(hit):
+    return jnp.where(hit, 1.0, 0.0).astype(BF)
+
+
+def pad_matrix(heads):
+    shape = (heads * HEAD_SIZE, heads * PAD)
+    row, col = iota(shape, 0), iota(shape, 1)
+    lane = col & 127
+    part = jnp.where(lane < 64, lane, lane - 16)
+    return one_hot((row == (col >> 7) * HEAD_SIZE + part) & ((lane & 63) < 48))
+
+
+def split_matrix():
+    row, col = iota((RUN, RUN), 0), iota((RUN, RUN), 1)
+    return one_hot(col == jnp.where(row < 128, 2 * row, 2 * row - 255))
+
+
+def merge_matrix():
+    row, col = iota((RUN, RUN), 0), iota((RUN, RUN), 1)
+    return one_hot(col == (row >> 1) + (row & 1) * 128)
+
+
+def rope_tables(run, cb_ref, sb_ref, cj_ref, sj_ref):
+    cb, sb = cb_ref[pl.ds(run, 1), :], sb_ref[pl.ds(run, 1), :]
+    cj, sj = cj_ref[...], sj_ref[...]
+    return cb * cj - sb * sj, sb * cj + cb * sj
+
+
+def rope(u, c, s):
+    return u * c + pltpu.roll(u, 64, 1) * s
+
+
+def rope_back(u, c, s):
+    return u * c - pltpu.roll(u, 64, 1) * s
+
+
+def vmem(*shape_dtype):
+    return pl.BlockSpec(memory_space=pltpu.VMEM)
+
+
+def entry_barrier(targets):
+    bar = pltpu.get_barrier_semaphore()
+    for t in targets:
+        pl.semaphore_signal(bar, inc=1, device_id=t, device_id_type=MESH)
+    pl.semaphore_wait(bar, len(targets))
+
+
+def remote(src, dst, send, recv, target):
+    return pltpu.make_async_remote_copy(
+        src_ref=src, dst_ref=dst, send_sem=send, recv_sem=recv, device_id=target, device_id_type=MESH
+    )
+
+
+def first_kernel(nc, x_ref, g_ref, cb_ref, sb_ref, cj_ref, sj_ref, wq_h, wk_h, wv_h, wo_h, wg_h, wu_h, wd_h,
+                 xp_ref, n1_ref, q_ref, kvp_ref, kvc_ref, wp_ref, gf_ref, wo_f, wg_f, wu_f, wd_f,
+                 wq_s, wk_s, wv_s, g_s, wo_v, wg_v, wu_v, wd_v, kv_send,
+                 lsem, ssem, rsem, osem, csem, crem):
+    s = lax.axis_index("shard")
+    c = lax.axis_index("context")
+    dh = g_s.shape[1] // 2
+    own = pl.ds(pl.multiple_of(s * dh, dh), dh)
+    other = {"shard": 1 - s}
+    loads = [
+        pltpu.make_async_copy(wq_h, wq_s.at[own], lsem.at[0]),
+        pltpu.make_async_copy(wk_h, wk_s.at[own], lsem.at[1]),
+        pltpu.make_async_copy(wv_h, wv_s.at[own], lsem.at[2]),
+        pltpu.make_async_copy(g_ref, g_s.at[:, own], lsem.at[3]),
+        pltpu.make_async_copy(wo_h, wo_v, lsem.at[4]),
+        pltpu.make_async_copy(wg_h, wg_v, lsem.at[5]),
+        pltpu.make_async_copy(wu_h, wu_v, lsem.at[6]),
+        pltpu.make_async_copy(wd_h, wd_v, lsem.at[7]),
+    ]
+    for cp in loads:
+        cp.start()
+    entry_barrier([other] + [{"context": lax.rem(c + i, nc)} for i in range(1, nc)])
+    sends = [
+        remote(wq_s.at[own], wq_s.at[own], ssem.at[0], rsem.at[0], other),
+        remote(wk_s.at[own], wk_s.at[own], ssem.at[1], rsem.at[1], other),
+        remote(wv_s.at[own], wv_s.at[own], ssem.at[2], rsem.at[2], other),
+        remote(g_s.at[:, own], g_s.at[:, own], ssem.at[3], rsem.at[3], other),
+        remote(wo_v, wo_f.at[:, own], ssem.at[4], rsem.at[4], other),
+        remote(wg_v, wg_f.at[own], ssem.at[5], rsem.at[5], other),
+        remote(wu_v, wu_f.at[own], ssem.at[6], rsem.at[6], other),
+        remote(wd_v, wd_f.at[:, own], ssem.at[7], rsem.at[7], other),
+    ]
+    keeps = [
+        pltpu.make_async_copy(wo_v, wo_f.at[:, own], osem.at[0]),
+        pltpu.make_async_copy(wg_v, wg_f.at[own], osem.at[1]),
+        pltpu.make_async_copy(wu_v, wu_f.at[own], osem.at[2]),
+        pltpu.make_async_copy(wd_v, wd_f.at[:, own], osem.at[3]),
+    ]
+    for i in (3, 0, 1, 2, 4, 5, 6, 7):
+        loads[i].wait()
+        sends[i].start()
+        if i >= 4:
+            keeps[i - 4].start()
+    half = x_ref.shape[0] // 2
+    split = split_matrix()
+    for i in range(x_ref.shape[0] // RUN):
+        xb = mm(split, x_ref[pl.ds(i * RUN, RUN), :])
+        xp_ref[pl.ds(i * 128, 128), :] = xb[:128].astype(BF)
+        xp_ref[pl.ds(half + i * 128, 128), :] = xb[128:].astype(BF)
+        if i == 0:
+            sends[3].wait_recv()
+        r = lax.rsqrt(jnp.mean(xb * xb, axis=-1, keepdims=True) + norm_eps)
+        nb = (xb * r * g_s[0:1, :]).astype(BF)
+        n1_ref[pl.ds(i * 128, 128), :] = nb[:128]
+        n1_ref[pl.ds(half + i * 128, 128), :] = nb[128:]
+    gf_ref[...] = g_s[...]
+    hq, hk = wq_s.shape[1] // HEAD_SIZE, wk_s.shape[1] // HEAD_SIZE
+    selq, selk = pad_matrix(hq), pad_matrix(hk)
+    nq, nk = hq * PAD, hk * PAD
+    for i in range(3):
+        sends[i].wait_recv()
+    for i in range(wq_s.shape[0] // RUN):
+        rows = pl.ds(i * RUN, RUN)
+        wp_ref[rows, 0:nq] = mm(wq_s[rows, :], selq).astype(BF)
+        wp_ref[rows, nq : nq + nk] = mm(wk_s[rows, :], selk).astype(BF)
+        wp_ref[rows, nq + nk :] = mm(wv_s[rows, :], selk).astype(BF)
+    selkv = pad_matrix(2 * hk)
+    runs = x_ref.shape[0] // RUN
+    per = runs // 2
+    kv_copies = []
+    for run in range(runs):
+        rows = pl.ds(run * RUN, RUN)
+        y = mm(n1_ref[rows, :], wp_ref[...])
+        ct, st = rope_tables(run, cb_ref, sb_ref, cj_ref, sj_ref)
+        for h in range(hq):
+            q_ref[rows, h * PAD : (h + 1) * PAD] = rope(y[:, h * PAD : (h + 1) * PAD], ct, st).astype(BF)
+        kv = [rope(y[:, nq + h * PAD : nq + (h + 1) * PAD], ct, st).astype(BF) for h in range(hk)]
+        kv = jnp.concatenate(kv + [y[:, nq + nk :].astype(BF)], axis=1)
+        if run < per:
+            kv_send[pl.ds(run * RUN, RUN), :] = mm_nt(kv, selkv).astype(BF)
+            mine = pl.ds(pl.multiple_of((c * per + run) * RUN, RUN), RUN)
+            for i in range(1, nc):
+                cp = remote(kv_send.at[pl.ds(run * RUN, RUN)], kvp_ref.at[mine], csem.at[run, i], crem.at[run, i],
+                            {"context": lax.rem(c + i, nc)})
+                cp.start()
+                kv_copies.append(cp)
+            cp = pltpu.make_async_copy(kv_send.at[pl.ds(run * RUN, RUN)], kvp_ref.at[mine], csem.at[run, 0])
+            cp.start()
+            kv_copies.append(cp)
+        else:
+            kvc_ref[pl.ds((run - per) * RUN, RUN), :] = kv
+    for cp in kv_copies:
+        cp.wait()
+    for i in range(4):
+        keeps[i].wait()
+        sends[4 + i].wait_recv()
+    for cp in sends:
+        cp.wait_send()
+
+
+def load_keys(kvp_ref, k_s, v_s, ones):
+    hk = k_s.shape[0]
+    sel = pad_matrix(2 * hk)
+    lane = iota((RUN, PAD), 1)
+
+    def step(i, _):
+        rows = pl.ds(pl.multiple_of(i * RUN, RUN), RUN)
+        kv = mm(kvp_ref[rows, :], sel)
+        for g in range(hk):
+            k_s[g, rows, :] = kv[:, g * PAD : (g + 1) * PAD].astype(BF)
+            v = kv[:, (hk + g) * PAD : (hk + g + 1) * PAD]
+            if ones:
+                v = jnp.where(lane == 48, 1.0, v)
+            v_s[g, rows, :] = v.astype(BF)
+        return 0
+
+    lax.fori_loop(0, kvp_ref.shape[0] // RUN, step, 0)
+
+
+def attend_kernel(kbase, qlim, q_ref, kvp_ref, kvc_ref, wo_ref, o_ref, op_ref, lse_ref, p_ref, k_s, v_s, s_s):
+    hk = k_s.shape[0]
+    hq = q_ref.shape[1] // PAD
+    rep = hq // hk
+    runs = q_ref.shape[0] // RUN
+    per = runs // 2
+    blocks = kvp_ref.shape[0] // RUN
+    scale = LOG2E / math.sqrt(HEAD_SIZE)
+    load_keys(kvp_ref, k_s, v_s, True)
+    lane = iota((RUN, PAD), 1)
+    diff = iota((RUN, RUN), 1) - iota((RUN, RUN), 0)
+
+    def head(run, h, own):
+        rows = pl.ds(pl.multiple_of(run * RUN, RUN), RUN)
+        cols = pl.ds(pl.multiple_of(h * PAD, PAD), PAD)
+        g = h // rep
+        q = q_ref[rows, cols]
+        lim = qlim[run]
+        top = None
+        for b in range(blocks):
+            s = mm_nt(q, k_s[g, pl.ds(b * RUN, RUN), :]) * scale
+            room = lim - kbase[b]
+            if own:
+                s = s + jnp.where(room >= 0, 0.0, NEG)
+            else:
+                s = jnp.where(diff <= room, s, NEG)
+            s_s[:, b * RUN : (b + 1) * RUN] = s
+            top = s if top is None else jnp.maximum(top, s)
+        if own:
+            crow = pl.ds(pl.multiple_of((run - per) * RUN, RUN), RUN)
+            kc = kvc_ref[crow, pl.ds(pl.multiple_of(g * PAD, PAD), PAD)]
+            vc = kvc_ref[crow, pl.ds(pl.multiple_of((hk + g) * PAD, PAD), PAD)]
+            vc = jnp.where(lane == 48, 1.0, vc.astype(F32)).astype(BF)
+            s = jnp.where(diff <= 0, mm_nt(q, kc) * scale, NEG)
+            s_s[:, blocks * RUN :] = s
+            top = jnp.maximum(top, s)
+        m = jnp.max(top, axis=1, keepdims=True)
+        acc = None
+        for b in range(blocks):
+            p = jnp.exp2(s_s[:, b * RUN : (b + 1) * RUN] - m).astype(BF)
+            o = mm(p, v_s[g, pl.ds(b * RUN, RUN), :])
+            acc = o if acc is None else acc + o
+        if own:
+            p = jnp.exp2(s_s[:, blocks * RUN :] - m).astype(BF)
+            acc = acc + mm(p, vc)
+        total = acc[:, 48:49]
+        op_ref[rows, cols] = (acc / total).astype(BF)
+        lse = jnp.broadcast_to(m + jnp.log2(total), (RUN, PAD)).T
+        lse_ref[pl.ds(pl.multiple_of((run * hq + h) * 8, 8), 8), :] = lse[0:8, :]
+
+    def prompt(i, _):
+        head(i // hq, lax.rem(i, hq), False)
+        return 0
+
+    def cont(i, _):
+        head(per + i // hq, lax.rem(i, hq), True)
+        return 0
+
+    lax.fori_loop(0, per * hq, prompt, 0)
+    lax.fori_loop(0, per * hq, cont, 0)
+    sel = pad_matrix(hq)
+
+    def project(i, _):
+        rows = pl.ds(pl.multiple_of(i * RUN, RUN), RUN)
+        o = mm_nt(op_ref[rows, :], sel).astype(BF)
+        o_ref[rows, :] = o
+        p_ref[rows, :] = mm(o, wo_ref[...]).astype(BF)
+        return 0
+
+    lax.fori_loop(0, runs, project, 0)
+
+
+def line_sum(n, chunk, pbuf, rbuf, obuf, rs, rr, bs, br):
+    z = lax.axis_index("tensor")
+    rows_half = pbuf.shape[0] // 2
+    count = rows_half // chunk
+    lag = 4
+
+    def pieces(h, i):
+        rows = pl.ds(pl.multiple_of(h * rows_half + i * chunk, chunk), chunk)
+        place = z if h == 0 else n - 1 - z
+        ahead = {"tensor": jnp.minimum(z + 1, n - 1) if h == 0 else jnp.maximum(z - 1, 0)}
+        back = {"tensor": jnp.maximum(z - 1, 0) if h == 0 else jnp.minimum(z + 1, n - 1)}
+        up = remote(pbuf.at[rows], rbuf.at[rows], rs.at[h, i], rr.at[h, i], ahead)
+        down = remote(obuf.at[rows], obuf.at[rows], bs.at[h, i], br.at[h, i], back)
+        return rows, place, up, down
+
+    def reduce_step(h, i):
+        rows, place, up, down = pieces(h, i)
+
+        @pl.when(place == 0)
+        def _():
+            up.start()
+
+        @pl.when(place > 0)
+        def _():
+            up.wait_recv()
+            total = (rbuf[rows, :].astype(F32) + pbuf[rows, :].astype(F32)).astype(BF)
+
+            @pl.when(place < n - 1)
+            def _():
+                pbuf[rows, :] = total
+                up.start()
+
+            @pl.when(place == n - 1)
+            def _():
+                obuf[rows, :] = total
+                down.start()
+
+    def spread_step(h, i):
+        rows, place, up, down = pieces(h, i)
+
+        @pl.when(place < n - 1)
+        def _():
+            down.wait_recv()
+
+        @pl.when((place < n - 1) & (place > 0))
+        def _():
+            down.start()
+
+    steps = count + (2 * (n - 1) * 4 + 2) // 3 + 1
+
+    def step(t, _):
+        for h in range(2):
+            place = z if h == 0 else n - 1 - z
+            i = t - (place * 4) // 3
+
+            @pl.when((i >= 0) & (i < count))
+            def _():
+                reduce_step(h, i)
+
+            j = t - ((2 * (n - 1) - place) * 4) // 3
+
+            @pl.when((j >= 0) & (j < count))
+            def _():
+                spread_step(h, j)
+
+        return 0
+
+    lax.fori_loop(0, steps, step, 0)
+
+    def finish(i, _):
+        for h in range(2):
+            rows, place, up, down = pieces(h, i)
+
+            @pl.when(place < n - 1)
+            def _():
+                up.wait_send()
+
+            @pl.when(place > 0)
+            def _():
+                down.wait_send()
+
+        return 0
+
+    lax.fori_loop(0, count, finish, 0)
+
+
+def line_barrier(n, peers=()):
+    z = lax.axis_index("tensor")
+    bar = pltpu.get_barrier_semaphore()
+    for t in peers:
+        pl.semaphore_signal(bar, inc=1, device_id=t, device_id_type=MESH)
+
+    @pl.when(z > 0)
+    def _():
+        pl.semaphore_signal(bar, inc=1, device_id={"tensor": jnp.maximum(z - 1, 0)}, device_id_type=MESH)
+
+    @pl.when(z < n - 1)
+    def _():
+        pl.semaphore_signal(bar, inc=1, device_id={"tensor": jnp.minimum(z + 1, n - 1)}, device_id_type=MESH)
+
+    pl.semaphore_wait(bar, len(peers) + jnp.minimum(z, 1) + jnp.minimum(n - 1 - z, 1))
+
+
+def sum_kernel(n, chunk, p_hbm, o_ref, pbuf, rbuf, lsem, rs, rr, bs, br):
+    cp = pltpu.make_async_copy(p_hbm, pbuf, lsem)
+    cp.start()
+    line_barrier(n)
+    cp.wait()
+    line_sum(n, chunk, pbuf, rbuf, o_ref, rs, rr, bs, br)
+
+
+def ffn_kernel(dy_ref, xp_ref, s1_ref, gf_ref, wg_ref, wu_ref, wd_ref,
+               dyp_ref, fp_ref, dn_ref, gg_ref, gu_ref, gd_ref,
+               n2_s, hid_s, dg_s, du_s):
+    rows_here = xp_ref.shape[0]
+    half = rows_here // 2
+    split = split_matrix()
+
+    def order(i, _):
+        b = mm(split, dy_ref[pl.ds(pl.multiple_of(i * RUN, RUN), RUN), :]).astype(BF)
+        dyp_ref[pl.ds(pl.multiple_of(i * 128, 128), 128), :] = b[:128]
+        dyp_ref[pl.ds(pl.multiple_of(half + i * 128, 128), 128), :] = b[128:]
+        return 0
+
+    lax.fori_loop(0, rows_here // RUN, order, 0)
+
+    def block(i, _):
+        rows = pl.ds(pl.multiple_of(i * RUN, RUN), RUN)
+        mid = xp_ref[rows, :].astype(F32) + s1_ref[rows, :].astype(F32)
+        r = lax.rsqrt(jnp.mean(mid * mid, axis=-1, keepdims=True) + norm_eps)
+        n2 = (mid * r * gf_ref[8:9, :]).astype(BF)
+        n2_s[rows, :] = n2
+        gate = mm(n2, wg_ref[...])
+        up = mm(n2, wu_ref[...])
+        sig = jax.nn.sigmoid(gate)
+        silu = gate * sig
+        hid = (silu * up).astype(BF)
+        hid_s[rows, :] = hid
+        fp_ref[rows, :] = mm(hid, wd_ref[...]).astype(BF)
+        dh = mm_nt(dyp_ref[rows, :], wd_ref[...])
+        dg = (dh * up * sig * (1.0 + gate * (1.0 - sig))).astype(BF)
+        du = (dh * silu).astype(BF)
+        dg_s[rows, :] = dg
+        du_s[rows, :] = du
+        dn_ref[rows, :] = (mm_nt(dg, wg_ref[...]) + mm_nt(du, wu_ref[...])).astype(BF)
+        return 0
+
+    lax.fori_loop(0, rows_here // RUN, block, 0)
+
+    def grads(i, _):
+        cols = pl.ds(pl.multiple_of(i * RUN, RUN), RUN)
+        nt = n2_s[:, cols].T
+        gg_ref[cols, :] = mm(nt, dg_s[...]).astype(BF)
+        gu_ref[cols, :] = mm(nt, du_s[...]).astype(BF)
+        return 0
+
+    lax.fori_loop(0, n2_s.shape[1] // RUN, grads, 0)
+    wide = dyp_ref.shape[1] // 2
+
+    def grads_down(i, _):
+        cols = pl.ds(pl.multiple_of(i * RUN, RUN), RUN)
+        ht = hid_s[:, cols].T
+        for s in range(2):
+            gd_ref[s, cols, :] = mm(ht, dyp_ref[:, s * wide : (s + 1) * wide]).astype(BF)
+        return 0
+
+    lax.fori_loop(0, hid_s.shape[1] // RUN, grads_down, 0)
+
+
+def back_kernel(kbase, qlim, cb_ref, sb_ref, cj_ref, sj_ref, dyp_ref, xp_ref, s1_ref, s2_ref, gf_ref, wo_ref, o_ref, op_ref,
+                lse_ref, q_ref, kvp_ref, kvc_ref,
+                dm_ref, g2_ref, go_ref, dqp_ref, dkvp_ref, dkvc_ref,
+                dmb_s, do_s, k_s, v_s, dk_s, dv_s):
+    hk = k_s.shape[0]
+    hq = q_ref.shape[1] // PAD
+    rep = hq // hk
+    rows_here = q_ref.shape[0]
+    runs = rows_here // RUN
+    per = runs // 2
+    blocks = kvp_ref.shape[0] // RUN
+    score = 1.0 / math.sqrt(HEAD_SIZE)
+    scale = LOG2E * score
+    load_keys(kvp_ref, k_s, v_s, False)
+    selq = pad_matrix(hq)
+    g2_ref[...] = jnp.zeros_like(g2_ref)
+
+    def middle(i, _):
+        rows = pl.ds(pl.multiple_of(i * RUN, RUN), RUN)
+        mid = xp_ref[rows, :].astype(F32) + s1_ref[rows, :].astype(F32)
+        r = lax.rsqrt(jnp.mean(mid * mid, axis=-1, keepdims=True) + norm_eps)
+        dn = s2_ref[rows, :].astype(F32)
+        w = gf_ref[8:9, :] * dn
+        inner = jnp.mean(w * mid, axis=-1, keepdims=True)
+        dm = dyp_ref[rows, :].astype(F32) + r * w - mid * (r * r * r) * inner
+        dm_ref[rows, :] = dm
+        g2_ref[...] += jnp.sum((dn * mid * r).reshape(RUN // 8, 8, mid.shape[1]), axis=0)
+        dmb = dm.astype(BF)
+        dmb_s[rows, :] = dmb
+        do = mm_nt(dmb, wo_ref[...]).astype(BF)
+        do_s[rows, :] = mm(do, selq).astype(BF)
+        return 0
+
+    lax.fori_loop(0, runs, middle, 0)
+    wide = dmb_s.shape[1] // 2
+    ot = o_ref[...].T
+    for s in range(2):
+        go_ref[s] = mm(ot, dmb_s[:, s * wide : (s + 1) * wide]).astype(BF)
+    dk_s[...] = jnp.zeros_like(dk_s)
+    dv_s[...] = jnp.zeros_like(dv_s)
+    width = rep * RUN
+    diff = iota((RUN, width), 0) - (iota((RUN, width), 1) & (RUN - 1))
+
+    def pair(run, g, own):
+        rows = pl.ds(pl.multiple_of(run * RUN, RUN), RUN)
+
+        def stack(ref):
+            parts = [ref[rows, pl.ds(pl.multiple_of((g * rep + j) * PAD, PAD), PAD)] for j in range(rep)]
+            return jnp.concatenate(parts, axis=0)
+
+        q, do, op = stack(q_ref), stack(do_s), stack(op_ref)
+        delta = jnp.sum((do.astype(F32) * op.astype(F32)).T, axis=0, keepdims=True)
+        lse = jnp.concatenate(
+            [lse_ref[pl.ds(pl.multiple_of((run * hq + g * rep + j) * 8, 8), 1), :] for j in range(rep)], axis=1
+        )
+        lim = qlim[run]
+
+        def tile(k, v, hide):
+            s = hide(mm_nt(k, q) * scale - lse)
+            p = jnp.exp2(s)
+            ds = (p * (mm_nt(v, do) - delta)).astype(BF)
+            return mm(ds, q), mm(p.astype(BF), do), mm_tn(ds, k)
+
+        dq = None
+        for b in range(blocks):
+            at = pl.ds(b * RUN, RUN)
+            room = lim - kbase[b]
+            if own:
+                hide = lambda s: s + jnp.where(room >= 0, 0.0, NEG)
+            else:
+                hide = lambda s: jnp.where(diff <= room, s, NEG)
+            dk, dv, d = tile(k_s[g, at, :], v_s[g, at, :], hide)
+            dk_s[g, at, :] += dk
+            dv_s[g, at, :] += dv
+            dq = d if dq is None else dq + d
+        ct, st = rope_tables(run, cb_ref, sb_ref, cj_ref, sj_ref)
+        if own:
+            crow = pl.ds(pl.multiple_of((run - per) * RUN, RUN), RUN)
+            kcol = pl.ds(pl.multiple_of(g * PAD, PAD), PAD)
+            vcol = pl.ds(pl.multiple_of((hk + g) * PAD, PAD), PAD)
+            hide = lambda s: jnp.where(diff <= 0, s, NEG)
+            dk, dv, d = tile(kvc_ref[crow, kcol], kvc_ref[crow, vcol], hide)
+            dq = dq + d
+            dkvc_ref[crow, kcol] = rope_back(dk * score, ct, st).astype(BF)
+            dkvc_ref[crow, vcol] = dv.astype(BF)
+        for j in range(rep):
+            part = rope_back(dq[j * RUN : (j + 1) * RUN] * score, ct, st)
+            dqp_ref[rows, pl.ds(pl.multiple_of((g * rep + j) * PAD, PAD), PAD)] = part.astype(BF)
+
+    def prompt(i, _):
+        pair(i // hk, lax.rem(i, hk), False)
+        return 0
+
+    def cont(i, _):
+        pair(per + i // hk, lax.rem(i, hk), True)
+        return 0
+
+    lax.fori_loop(0, per * hk, prompt, 0)
+    lax.fori_loop(0, per * hk, cont, 0)
+    selkv = pad_matrix(2 * hk)
+
+    def pack(i, _):
+        rows = pl.ds(pl.multiple_of(i * RUN, RUN), RUN)
+        parts = [(dk_s[g, rows, :] * score).astype(BF) for g in range(hk)]
+        parts += [dv_s[g, rows, :].astype(BF) for g in range(hk)]
+        dkvp_ref[rows, :] = mm_nt(jnp.concatenate(parts, axis=1), selkv).astype(BF)
+        return 0
+
+    lax.fori_loop(0, blocks, pack, 0)
+
+
+def keys_kernel(nc, cb_ref, sb_ref, cj_ref, sj_ref, dkvp_ref, dkvc_ref, dqp_ref, n1_ref, wp_ref, dn_ref, gw_ref,
+                recv, dkv_s, ssem, rsem):
+    c = lax.axis_index("context")
+    rows_here = dqp_ref.shape[0]
+    half = rows_here // 2
+    entry_barrier([{"context": lax.rem(c + i, nc)} for i in range(1, nc)])
+    copies = []
+    for i in range(1, nc):
+        to = lax.rem(c + i, nc)
+        cp = remote(dkvp_ref.at[pl.ds(pl.multiple_of(to * half, half), half)], recv.at[i - 1], ssem.at[i - 1], rsem.at[i - 1],
+                    {"context": to})
+        cp.start()
+        copies.append(cp)
+    nq = dqp_ref.shape[1]
+    nkv = dkvc_ref.shape[1]
+    hk = nkv // PAD // 2
+    hq = nq // PAD
+    selq, selkv = pad_matrix(hq), pad_matrix(2 * hk)
+    nt_rows = n1_ref.shape[1]
+    dq_u = mm_nt(dqp_ref[...], selq).astype(BF)
+    wide_q = hq * HEAD_SIZE
+
+    def grads_q(i, _):
+        cols = pl.ds(pl.multiple_of(i * RUN, RUN), RUN)
+        gw_ref[cols, 0:wide_q] = mm(n1_ref[:, cols].T, dq_u).astype(BF)
+        return 0
+
+    lax.fori_loop(0, nt_rows // RUN, grads_q, 0)
+    for cp in copies:
+        cp.wait_recv()
+    for run in range(half // RUN):
+        rows = pl.ds(run * RUN, RUN)
+        mine = pl.ds(pl.multiple_of(c * half + run * RUN, RUN), RUN)
+        total = mm(dkvp_ref[mine, :], selkv)
+        for i in range(nc - 1):
+            total = total + mm(recv[i, rows, :], selkv)
+        ct, st = rope_tables(run, cb_ref, sb_ref, cj_ref, sj_ref)
+        for g in range(hk):
+            dkv_s[rows, g * PAD : (g + 1) * PAD] = rope_back(total[:, g * PAD : (g + 1) * PAD], ct, st).astype(BF)
+        dkv_s[rows, hk * PAD :] = total[:, hk * PAD :].astype(BF)
+    dkv_s[pl.ds(half, half), :] = dkvc_ref[...]
+    dkv_u = mm_nt(dkv_s[...], selkv).astype(BF)
+
+    def grads_kv(i, _):
+        cols = pl.ds(pl.multiple_of(i * RUN, RUN), RUN)
+        gw_ref[cols, wide_q:] = mm(n1_ref[:, cols].T, dkv_u).astype(BF)
+        return 0
+
+    lax.fori_loop(0, nt_rows // RUN, grads_kv, 0)
+
+    def normed(i, _):
+        rows = pl.ds(pl.multiple_of(i * RUN, RUN), RUN)
+        dn = mm_nt(dqp_ref[rows, :], wp_ref[:, 0:nq]) + mm_nt(dkv_s[rows, :], wp_ref[:, nq:])
+        dn_ref[rows, :] = dn.astype(BF)
+        return 0
+
+    lax.fori_loop(0, rows_here // RUN, normed, 0)
+    for cp in copies:
+        cp.wait_send()
+
+
+def last_kernel(n, nc, chunk, fp_h, dn_h, xp_ref, s1_ref, dm_ref, gf_ref, g2_ref, out_ref, tg_ref, gg_ref,
+                pbuf, rbuf, obuf, gpart, grecv, lsem, rs, rr, bs, br, gs, gr):
+    rows_here = xp_ref.shape[0]
+    half = rows_here // 2
+    s = lax.axis_index("shard")
+    c = lax.axis_index("context")
+    loads = [pltpu.make_async_copy(fp_h, pbuf.at[pl.ds(0, rows_here)], lsem.at[0]),
+             pltpu.make_async_copy(dn_h, pbuf.at[pl.ds(rows_here, rows_here)], lsem.at[1])]
+    for cp in loads:
+        cp.start()
+    peers = []
+    for i in range(1, 2 * nc):
+        peers.append({"shard": lax.rem(s + i // nc, 2), "context": lax.rem(c + lax.rem(i, nc), nc)})
+    line_barrier(n, peers)
+    for cp in loads:
+        cp.wait()
+    line_sum(n, chunk, pbuf, rbuf, obuf, rs, rr, bs, br)
+    merge = merge_matrix()
+    gpart[0:8, :] = jnp.zeros((8, gpart.shape[1]), F32)
+    gpart[8:16, :] = g2_ref[...]
+
+    def block(i, _):
+        a = pl.ds(pl.multiple_of(i * 128, 128), 128)
+        b = pl.ds(pl.multiple_of(half + i * 128, 128), 128)
+
+        def take(ref, base=0):
+            lo = ref[pl.ds(pl.multiple_of(base + i * 128, 128), 128), :]
+            hi = ref[pl.ds(pl.multiple_of(base + half + i * 128, 128), 128), :]
+            return jnp.concatenate([lo, hi], axis=0).astype(F32)
+
+        x = take(xp_ref)
+        mid = x + take(s1_ref)
+        rows = pl.ds(pl.multiple_of(i * RUN, RUN), RUN)
+        out_ref[rows, :] = mm(merge, (mid + take(obuf)).astype(BF)).astype(BF)
+        dn = take(obuf, rows_here)
+        r = lax.rsqrt(jnp.mean(x * x, axis=-1, keepdims=True) + norm_eps)
+        w = gf_ref[0:1, :] * dn
+        inner = jnp.mean(w * x, axis=-1, keepdims=True)
+        tg = take(dm_ref) + (r * w - x * (r * r * r) * inner)
+        tg_ref[rows, :] = mm(merge, tg.astype(BF)).astype(BF)
+        gpart[0:8, :] += jnp.sum((dn * x * r).reshape(RUN // 8, 8, x.shape[1]), axis=0)
+        return 0
+
+    lax.fori_loop(0, rows_here // RUN, block, 0)
+    me = s * nc + c
+    sums = jnp.concatenate(
+        [jnp.broadcast_to(jnp.sum(gpart[k * 8 : (k + 1) * 8, :], axis=0, keepdims=True), (8, gpart.shape[1])) for k in range(2)], axis=0
+    )
+    grecv[me] = sums
+    copies = []
+    for i, t in enumerate(peers):
+        cp = remote(grecv.at[me], grecv.at[me], gs.at[i], gr.at[i], t)
+        cp.start()
+        copies.append(cp)
+    for cp in copies:
+        cp.wait()
+    total = grecv[0]
+    for i in range(1, 2 * nc):
+        total = total + grecv[i]
+    gg_ref[...] = total
+
+
+def fast(
+    tokens, w_query, key_weight, value_weight, w_out, w_gate, w_up, w_down, gain_attn, gain_ffn, segments, positions, cotangent, n, nc
+):
+    _, rows, d = tokens.shape
+    half = rows // 2
+    runs = rows // RUN
+    per = runs // 2
+    prompt = segments.shape[1] // 2
+    blocks = prompt // RUN
+    dq, dk = w_query.shape[1], key_weight.shape[1]
+    hq, hk = dq // HEAD_SIZE, dk // HEAD_SIZE
+    nq, nk = hq * PAD, hk * PAD
+    ff = w_gate.shape[1]
+    dh = d // 2
+    c = lax.axis_index("context")
+    x = tokens.reshape(rows, d)
+    dy = cotangent.reshape(rows, d)
+    kbase = positions[0, 0 :: 2 * RUN]
+    seg_here = lax.dynamic_slice_in_dim(segments[0], c * rows, rows, 0)
+    pos_here = lax.dynamic_slice_in_dim(positions[0], c * rows, rows, 0)
+    qbase = jnp.concatenate([pos_here[0 :: 2 * RUN], pos_here[1 :: 2 * RUN]])
+    qlim = jnp.concatenate([pos_here[0 :: 2 * RUN], seg_here[1 :: 2 * RUN] * CLEN - 1])
+    freq = np.exp(np.arange(HEAD_SIZE // 2, dtype=np.float32) * np.float32(-2.0 * math.log(rope_base) / HEAD_SIZE)).astype(np.float32)
+    lanes = np.zeros((PAD,), np.float32)
+    lanes[0:48] = freq
+    lanes[64:112] = freq
+    sign = np.where(np.arange(PAD) < 64, -1.0, 1.0).astype(np.float32)
+    inner = np.arange(RUN, dtype=np.float64)[:, None] * lanes[None, :].astype(np.float64)
+    cj = jnp.asarray(np.cos(inner).astype(np.float32))
+    sj = jnp.asarray((np.sin(inner) * sign).astype(np.float32))
+    angle = qbase.astype(F32)[:, None] * jnp.asarray(lanes)[None, :]
+    cb = jnp.cos(angle)
+    sb = jnp.sin(angle) * jnp.asarray(sign)[None, :]
+    gains = jnp.concatenate([jnp.broadcast_to(g.astype(F32)[None, :], (8, dh)) for g in (gain_attn, gain_ffn)], axis=0)
+
+    V = pl.BlockSpec(memory_space=pltpu.VMEM)
+    S = pl.BlockSpec(memory_space=pltpu.SMEM)
+    A = pl.BlockSpec(memory_space=pl.ANY)
+    sds = jax.ShapeDtypeStruct
+    DMA = pltpu.SemaphoreType.DMA
+
+    def call(kernel, ins, outs, scratch, collective=None, flops=0):
+        params = dict(vmem_limit_bytes=VLIM - 64 * 1024)
+        if collective is not None:
+            params.update(collective_id=collective, has_side_effects=True)
+        args = [a for a, _ in ins]
+        return pl.pallas_call(
+            kernel,
+            out_shape=[o for o, _ in outs],
+            in_specs=[sp for _, sp in ins],
+            out_specs=[sp for _, sp in outs],
+            scratch_shapes=scratch,
+            compiler_params=pltpu.CompilerParams(**params),
+            cost_estimate=pl.CostEstimate(flops=flops, bytes_accessed=0, transcendentals=0),
+        )(*args)
+
+    rope_in = [(cb, V), (sb, V), (cj, V), (sj, V)]
+    xp, n1, q, kvp, kvc, wp, gf, wo, wg, wu, wd = call(
+        functools.partial(first_kernel, nc),
+        [(x, V), (gains, A)] + rope_in + [(w_query, A), (key_weight, A), (value_weight, A), (w_out, A), (w_gate, A), (w_up, A), (w_down, A)],
+        [
+            (sds((rows, d), BF), V), (sds((rows, d), BF), V), (sds((rows, nq), BF), V),
+            (sds((prompt, 2 * dk), BF), A), (sds((half, 2 * nk), BF), V), (sds((d, nq + 2 * nk), BF), V), (sds((16, d), F32), V),
+            (sds((dq, d), BF), A), (sds((d, ff), BF), A), (sds((d, ff), BF), A), (sds((ff, d), BF), A),
+        ],
+        [
+            pltpu.VMEM((d, dq), BF), pltpu.VMEM((d, dk), BF), pltpu.VMEM((d, dk), BF), pltpu.VMEM((16, d), F32),
+            pltpu.VMEM((dq, dh), BF), pltpu.VMEM((dh, ff), BF), pltpu.VMEM((dh, ff), BF), pltpu.VMEM((ff, dh), BF),
+            pltpu.VMEM((half, 2 * dk), BF),
+            DMA((8,)), DMA((8,)), DMA((8,)), DMA((4,)), DMA((per, nc)), DMA((per, nc)),
+        ],
+        collective=0, flops=60 * 10**9,
+    )
+    o, op, lse, part = call(
+        attend_kernel,
+        [(kbase, S), (qlim, S), (q, V), (kvp, V), (kvc, V), (wo, V)],
+        [(sds((rows, dq), BF), V), (sds((rows, nq), BF), V), (sds((runs * hq * 8, RUN), F32), V), (sds((rows, d), BF), V)],
+        [pltpu.VMEM((hk, prompt, PAD), BF), pltpu.VMEM((hk, prompt, PAD), BF), pltpu.VMEM((RUN, prompt + RUN), F32)],
+        flops=60 * 10**9,
+    )
+
+    def line(part, collective):
+        r = part.shape[0]
+        chunk = 32
+        count = r // 2 // chunk
+        return call(
+            functools.partial(sum_kernel, n, chunk), [(part, A)], [(sds((r, d), BF), V)],
+            [pltpu.VMEM((r, d), BF), pltpu.VMEM((r, d), BF), DMA] + [DMA((2, count))] * 4,
+            collective=collective, flops=80 * 10**9,
+        )[0]
+
+    s1 = line(part, 1)
+    dyp, fp, dn2, gg, gu, gd = call(
+        ffn_kernel,
+        [(dy, V), (xp, V), (s1, V), (gf, V), (wg, V), (wu, V), (wd, V)],
+        [(sds((rows, d), BF), V)] * 3 + [(sds((d, ff), BF), V), (sds((d, ff), BF), V), (sds((2, ff, dh), BF), V)],
+        [pltpu.VMEM((rows, d), BF), pltpu.VMEM((rows, ff), BF), pltpu.VMEM((rows, ff), BF), pltpu.VMEM((rows, ff), BF)],
+        flops=60 * 10**9,
+    )
+    both = ("shard", "context")
+
+    def reduce_rows(g):
+        g = lax.psum_scatter(g, both, scatter_dimension=0, tiled=True)
+        return lax.all_gather(g, "context", axis=0, tiled=True)
+
+    gg, gu, gd = reduce_rows(gg), reduce_rows(gu), reduce_rows(gd.reshape(2 * ff, dh))
+    s2 = line(dn2, 2)
+    dm, g2, go, dqp, dkvp, dkvc = call(
+        back_kernel,
+        [(kbase, S), (qlim, S)] + rope_in + [(dyp, V), (xp, V), (s1, V), (s2, V), (gf, V), (wo, V), (o, V), (op, V), (lse, V), (q, V), (kvp, V), (kvc, V)],
+        [
+            (sds((rows, d), F32), V), (sds((8, d), F32), V), (sds((2, dq, dh), BF), V), (sds((rows, nq), BF), V),
+            (sds((prompt, 2 * dk), BF), V), (sds((half, 2 * nk), BF), V),
+        ],
+        [
+            pltpu.VMEM((rows, d), BF), pltpu.VMEM((rows, nq), BF), pltpu.VMEM((hk, prompt, PAD), BF), pltpu.VMEM((hk, prompt, PAD), BF),
+            pltpu.VMEM((hk, prompt, PAD), F32), pltpu.VMEM((hk, prompt, PAD), F32),
+        ],
+        flops=100 * 10**9,
+    )
+    go = reduce_rows(go.reshape(2 * dq, dh))
+    dn1, gw = call(
+        functools.partial(keys_kernel, nc),
+        rope_in + [(dkvp, V), (dkvc, V), (dqp, V), (n1, V), (wp, V)],
+        [(sds((rows, d), BF), V), (sds((d, dq + 2 * dk), BF), V)],
+        [pltpu.VMEM((nc - 1, half, 2 * dk), BF), pltpu.VMEM((rows, 2 * nk), BF), DMA((nc - 1,)), DMA((nc - 1,))],
+        collective=3, flops=40 * 10**9,
+    )
+    gw = reduce_rows(gw)
+    chunk = 32
+    count = rows // chunk
+    out, tg, gains_grad = call(
+        functools.partial(last_kernel, n, nc, chunk),
+        [(fp, A), (dn1, A), (xp, V), (s1, V), (dm, V), (gf, V), (g2, V)],
+        [(sds((rows, d), BF), V), (sds((rows, d), BF), V), (sds((16, d), F32), V)],
+        [
+            pltpu.VMEM((2 * rows, d), BF), pltpu.VMEM((2 * rows, d), BF), pltpu.VMEM((2 * rows, d), BF),
+            pltpu.VMEM((16, d), F32), pltpu.VMEM((2 * nc, 16, d), F32), DMA((2,)),
+        ]
+        + [DMA((2, count))] * 4
+        + [DMA((2 * nc - 1,)), DMA((2 * nc - 1,))],
+        collective=4, flops=160 * 10**9,
+    )
+    s = lax.axis_index("shard")
+    g1o = lax.dynamic_slice_in_dim(gains_grad[0], s * dh, dh, 0)
+    g2o = lax.dynamic_slice_in_dim(gains_grad[8], s * dh, dh, 0)
+    return (
+        out[None], tg[None],
+        gw[:, :dq].astype(F32), gw[:, dq : dq + dk].astype(F32), gw[:, dq + dk :].astype(F32),
+        go.astype(F32), gg.astype(F32), gu.astype(F32), gd.astype(F32), g1o, g2o,
+    )
+
+
+def body(mesh, *args):
+    tokens, w_query, segments = args[0], args[1], args[10]
+    n, nc = mesh.shape["tensor"], mesh.shape["context"]
+    rows = tokens.shape[1]
+    if (tokens.shape[0] == 1 and rows % (4 * CLEN) == 0 and n > 1 and nc > 1 and mesh.shape["shard"] == 2
+            and segments.shape[1] == rows * nc):
+        return fast(*args, n, nc)
+    return general(*args)
+
+
 def solution(mesh):
     in_specs = (
         P("shard", "context", None),
@@ -390,4 +1230,4 @@
         P("shard"),
         P("shard"),
     )
-    return jax.shard_map(body, mesh=mesh, in_specs=in_specs, out_specs=out_specs, check_vma=False)
+    return jax.shard_map(functools.partial(body, mesh), mesh=mesh, in_specs=in_specs, out_specs=out_specs, check_vma=False)

time: 1620 us -> 807 us (0.50)
  waiting for transfers between devices: 1060 us -> 206 us
  Pallas kernels: 0 us -> 535 us
  matrix products: 261 us -> 0 us
  other arithmetic: 156 us -> 16.6 us
  blocking collectives: 74.8 us -> 10.1 us
  local copies, waits for them, and re-layouts: 36.4 us -> 16.3 us
    psum x4 -> x0, waiting for transfers between devices: 734 us -> none  [the longest x1 219 us: body(): lax.psum(jnp.dot(attended_low, w_out, preferred_element_type=jnp.float32)...]
    pallas_call x0 -> x8, Pallas kernels: none -> 535 us  [call(): pl.pallas_call(kernel, out_shape=[o for o, _ in outs], in_specs=[sp for _...]
    dot_general x27 -> x0, matrix products: 261 us -> none  [the longest x1 45.7 us: attend_back(): jnp.einsum('bhgd,khd->hgbk', grad_grouped, value_head_rows, preferred_ele...]
    all_gather x9 -> x4, waiting for transfers between devices: 123 us -> 0.01 us  [reduce_rows(): return lax.all_gather(g, 'context', axis=0, tiled=True)]
    convert_element_type x19 -> x6, other arithmetic: 77.3 us -> 14 us  [the longest x1 3.61 us: fast(): gg.astype(F32)]
    reduce_sum x5 -> x0, other arithmetic: 38.2 us -> none  [the longest x1 21.2 us: attend_group(): totals = jnp.sum(exponent, axis=-1, keepdims=True)]
    unnamed x2 -> x0, blocking collectives: 33.1 us -> none
    all_gather x8 -> x1, blocking collectives: 41.6 us -> 10.1 us  [reduce_rows(): return lax.all_gather(g, 'context', axis=0, tiled=True)]
  transfers between devices with their start and end apart: 21 -> 9, of which waited for: 16 -> 4; matrix products, arithmetic and copies ran while one was open for 25% -> 2% of each run, Pallas kernels for 0% -> 23%
where the time goes in v1:
time: 807 us; the launch traced here: 798 us
  Pallas kernels  535 us (66%)
  waiting for transfers between devices  206 us (26%)
  other arithmetic  16.6 us (2%)
  local copies, waits for them, and re-layouts  16.3 us (2%)
  between operations  14.4 us (2%)
  blocking collectives  10.1 us (1%)
    pallas_call x8, Pallas kernels, call(): pl.pallas_call(kernel, out_shape=[o for o, _ in outs], in_specs=[sp for _...  535 us
    reduce_scatter x5, waiting for transfers between devices, reduce_rows(): g = lax.psum_scatter(g, both, scatter_dimension=0, tiled=True)  203 us
  transfers between devices with their start and end apart: 9, of which 4 were waited for; matrix products, arithmetic and copies ran while one was open for 2% of the time, Pallas kernels for 23%

profile of v1, /device:TPU:1, one launch (start us, length us, event | category | flops | bytes accessed | tf_op | source)
XLA Modules:
  0.0 798.3 jit_solution(7134780546177270175)
XLA Ops:
  7.2 1.3 slice.30
  9.5 1.9 copy.28.wk_h
  11.4 1.9 copy.29.wv_h
  15.9 1.4 fusion
  17.2 34.0 %shard_map.248 = (bf16[1024,1536]{1,0:T(8,128)(2,1)}, bf16[1024,1536]{1,0:T(8,128)(2,1)}, bf16[1024,512]{1,0:T(8,128)(2,1)}, bf16[2048,384]{1,0:T(8,128)(2,1)}, ...) custom-call(bf16[1024,1536]{1,0:T(8,128)(2,1)} %bitcast.16, ...), custom_call_target="tpu_custom_call" | custom-call | flops 60000002048 | tf_op jit(solution)/shard_map/pallas_call | solution.py:1087
  51.2 27.5 %shard_map.249 = (bf16[1024,384]{1,0:T(8,128)(2,1)}, bf16[1024,512]{1,0:T(8,128)(2,1)}, f32[128,256]{1,0:T(8,128)}, bf16[1024,1536]{1,0:T(8,128)(2,1)}) custom-call(s32[8]{0:T(128)} %bitcast.18, s32[4]{0:T(128)} %get-tuple-element.92.qlim, bf16[1024,512]{1,0:T(8,128)(2,1)} %get-tuple-element.44.q_ref, bf16[2048,384]{1,0:T(8,128)(2,1)} %get-tuple-element.45.kvp_ref, ...), custom_call_target="tpu_custom_call" | custom-call | flops 60000002048 | tf_op jit(solution)/shard_map/pallas_call | solution.py:1087
  78.8 80.8 %shard_map.250.s1_ref = bf16[1024,1536]{1,0:T(8,128)(2,1)} custom-call(bf16[1024,1536]{1,0:T(8,128)(2,1)} %get-tuple-element.48.p_hbm), custom_call_target="tpu_custom_call" | custom-call | flops 80000000000 | tf_op jit(solution)/shard_map/pallas_call | solution.py:1087
  159.6 47.9 %shard_map.251 = (bf16[1024,1536]{1,0:T(8,128)(2,1)}, bf16[1024,1536]{1,0:T(8,128)(2,1)}, bf16[1024,1536]{1,0:T(8,128)(2,1)}, bf16[1536,1024]{1,0:T(8,128)(2,1)}...) custom-call(bf16[1024,1536]{1,0:T(8,128)(2,1)} %bitcast.17, bf16[1024,1536]{1,0:T(8,128)(2,1)} %get-tuple-element.43.xp_ref, ...), custom_call_target="tpu_custom_call" | custom-call | flops 60000002048 | tf_op jit(solution)/shard_map/pallas_call | solution.py:1087
  207.5 80.4 %shard_map.252.s2_ref = bf16[1024,1536]{1,0:T(8,128)(2,1)} custom-call(bf16[1024,1536]{1,0:T(8,128)(2,1)} %get-tuple-element.55.p_hbm), custom_call_target="tpu_custom_call" | custom-call | flops 80000000000 | tf_op jit(solution)/shard_map/pallas_call | solution.py:1087
  287.9 53.3 %shard_map.253 = (f32[1024,1536]{1,0:T(8,128)}, f32[8,1536]{1,0:T(8,128)}, bf16[2,384,768]{2,1,0:T(8,128)(2,1)}, bf16[1024,512]{1,0:T(8,128)(2,1)}, bf16[2048,384]{1,0:T(8,128)(2,1)}, /*index=5*/bf16[512,512]{1,0:T(8,128)(2,1)}) custom-call(s32[8]{0:T(128)} %bitcast.19, s32[4]{0:T(128)} %get-tuple-element.92.qlim, f32[4,128]{1,0:T(4,128)} %get-tuple-element.91.cb_ref, ...), custom_call_target="tpu_custom_call" | custom-call | flops 99999997952 | tf_op jit(solution)/shard_map/pallas_call | solution.py:1087
  341.1 29.7 %shard_map.254 = (bf16[1024,1536]{1,0:T(8,128)(2,1)}, bf16[1536,768]{1,0:T(8,128)(2,1)}) custom-call(f32[4,128]{1,0:T(4,128)} %get-tuple-element.91.cb_ref, f32[4,128]{1,0:T(4,128)} %get-tuple-element.90.sb_ref, f32[256,128]{1,0:T(8,128)} %constant.38.clone.cj_ref, f32[256,128]{1,0:T(8,128)} %constant.39.clone.sj_ref, ...), custom_call_target="tpu_custom_call" | custom-call | flops 40000000000 | tf_op jit(solution)/shard_map/pallas_call | solution.py:1087
  373.6 54.2 %reduce-scatter.6.cloned.1.call-done = bf16[192,768]{1,0:T(8,128)(2,1)} async-done(((bf16[1536,768]{1,0:T(8,128)(2,1)}), bf16[192,768]{1,0:T(8,128)(2,1)}) %reduce-scatter.6.cloned.1.call-update) | async-done | bytes 294928 | tf_op jit(solution)/shard_map/reduce_scatter | solution.py:1143
  427.8 49.4 %reduce-scatter.14.cloned.1.call-done = bf16[256,768]{1,0:T(8,128)(2,1)} async-done(((bf16[2048,768]{1,0:T(8,128)(2,1)}), bf16[256,768]{1,0:T(8,128)(2,1)}) %reduce-scatter.14.cloned.1.call-update) | async-done | bytes 393232 | tf_op jit(solution)/shard_map/reduce_scatter | solution.py:1143
  477.3 50.0 %reduce-scatter.12.cloned.1.call-done = bf16[192,1024]{1,0:T(8,128)(2,1)} async-done(((bf16[1536,1024]{1,0:T(8,128)(2,1)}), bf16[192,1024]{1,0:T(8,128)(2,1)}) %reduce-scatter.12.cloned.1.call-update) | async-done | bytes 393232 | tf_op jit(solution)/shard_map/reduce_scatter | solution.py:1143
  527.3 49.8 %reduce-scatter.10.cloned.1.call-done = bf16[192,1024]{1,0:T(8,128)(2,1)} async-done(((bf16[1536,1024]{1,0:T(8,128)(2,1)}), bf16[192,1024]{1,0:T(8,128)(2,1)}) %reduce-scatter.10.cloned.1.call-update) | async-done | bytes 393232 | tf_op jit(solution)/shard_map/reduce_scatter | solution.py:1143
  577.2 181.2 %shard_map.255 = (bf16[1024,1536]{1,0:T(8,128)(2,1)}, bf16[1024,1536]{1,0:T(8,128)(2,1)}, f32[16,1536]{1,0:T(8,128)}) custom-call(bf16[1024,1536]{1,0:T(8,128)(2,1)} %get-tuple-element.53.fp_h, bf16[1024,1536]{1,0:T(8,128)(2,1)} %get-tuple-element.64.dn_h, bf16[1024,1536]{1,0:T(8,128)(2,1)} %get-tuple-element.43.xp_ref, ...), custom_call_target="tpu_custom_call" | custom-call | flops 160000000000 | tf_op jit(solution)/shard_map/pallas_call | solution.py:1087
  760.4 10.1 %all_gather.16 = bf16[384,768]{1,0:T(8,128)(2,1)S(1)} all-gather(bf16[96,768]{1,0:T(8,128)(2,1)} %reduce-scatter.8.cloned.1.call-done), channel_id=1, replica_groups=mesh['shard'=2,'context'=4,'tensor'=4] {'context'}, dimensions={0}, use_global_device_ids=true | all-gather | bytes 737280 | tf_op jit(solution)/shard_map/all_gather | solution.py:1144
  771.6 1.4 slice_convert_fusion.1
  776.2 3.3 convert_element_type.43
  779.5 3.5 convert_element_type.42
  783.0 3.6 convert_element_type.41
  786.6 1.7 copy.34
  788.3 1.4 copy-done
  789.7 1.7 copy.35
  (44 shorter events, 12.8 us)
Async XLA Ops:
  7.2 420.6 %reduce-scatter.6.cloned.1.call-start = ((), (), s32[]{:S(2)}) async-start(), calls=%async_computation.5 | async-start | bytes 2654208 | tf_op jit(solution)/shard_map/reduce_scatter | solution.py:1143
  370.9 106.3 %reduce-scatter.14.cloned.1.call-start = ((), (), s32[]{:S(2)}) async-start(), calls=%async_computation.12 | async-start | bytes 3538944 | tf_op jit(solution)/shard_map/reduce_scatter | solution.py:1143
  371.6 155.6 %reduce-scatter.12.cloned.1.call-start = ((), (), s32[]{:S(2)}) async-start(), calls=%async_computation.10 | async-start | bytes 3538944 | tf_op jit(solution)/shard_map/reduce_scatter | solution.py:1143
  372.4 204.8 %reduce-scatter.10.cloned.1.call-start = ((), (), s32[]{:S(2)}) async-start(), calls=%async_computation.8 | async-start | bytes 3538944 | tf_op jit(solution)/shard_map/reduce_scatter | solution.py:1143
  372.9 387.5 %reduce-scatter.8.cloned.1.call-start = ((), (), s32[]{:S(2)}) async-start(), calls=%async_computation.7 | async-start | bytes 1327104 | tf_op jit(solution)/shard_map/reduce_scatter | solution.py:1143
  373.5 398.1 %all-gather.5.cloned.1.call-start = ((), (), s32[]{:S(2)}) async-start(), calls=%async_computation.6 | async-start | bytes 1474560 | tf_op jit(solution)/shard_map/all_gather | solution.py:1144
  427.8 348.5 %all-gather.11.cloned.1.call-start = ((), (), s32[]{:S(2)}) async-start(), calls=%async_computation.13 | async-start | bytes 1966080 | tf_op jit(solution)/shard_map/all_gather | solution.py:1144
  477.2 302.3 %all-gather.9.cloned.1.call-start = ((), (), s32[]{:S(2)}) async-start(), calls=%async_computation.11 | async-start | bytes 1966080 | tf_op jit(solution)/shard_map/all_gather | solution.py:1144
  527.3 255.7 %all-gather.7.cloned.1.call-start = ((), (), s32[]{:S(2)}) async-start(), calls=%async_computation.9 | async-start | bytes 1966080 | tf_op jit(solution)/shard_map/all_gather | solution.py:1144
  771.6 3.6 copy-start.2
  783.0 3.6 copy-start.1
  786.6 3.0 copy-start
Sparse Core Ops, SparseCore 0:
  371.0 56.6 reduce-scatter.5
  431.1 46.0 reduce-scatter.13
  481.2 46.0 reduce-scatter.11
  531.0 46.0 reduce-scatter.9
  580.8 36.5 reduce-scatter.7
  619.0 27.7 all-gather.4
  648.6 30.8 all-gather.10
  681.3 30.8 all-gather.8
  714.1 37.7 all-gather.6

commit v2 on v0

--- a/solution.py
+++ b/solution.py
@@ -1,8 +1,12 @@
+import functools
 import math
 
 import jax
 import jax.numpy as jnp
+import numpy as np
 from jax import lax
+from jax.experimental import pallas as pl
+from jax.experimental.pallas import tpu as pltpu
 from jax.sharding import PartitionSpec as P
 
 HEAD_SIZE = 96
@@ -78,7 +82,7 @@
     return own | branch
 
 
-def body(
+def general(
     tokens,
     w_query,
     key_weight,
@@ -361,6 +365,1146 @@
     )
 
 
+MESH = pl.DeviceIdType.MESH
+RUN = 256
+PAD = 128
+NEG = -1e30
+LOG2E = 1.4426950408889634
+BF = jnp.bfloat16
+F32 = jnp.float32
+VLIM = 64 * 1024 * 1024
+
+
+def mm(a, b):
+    return lax.dot_general(a, b, (((1,), (0,)), ((), ())), preferred_element_type=F32)
+
+
+def mm_nt(a, b):
+    return lax.dot_general(a, b, (((1,), (1,)), ((), ())), preferred_element_type=F32)
+
+
+def mm_tn(a, b):
+    return lax.dot_general(a, b, (((0,), (0,)), ((), ())), preferred_element_type=F32)
+
+
+def iota(shape, axis):
+    return lax.broadcasted_iota(jnp.int32, shape, axis)
+
+
+def one_hot(hit):
+    return jnp.where(hit, 1.0, 0.0).astype(BF)
+
+
+def pad_matrix(heads):
+    shape = (heads * HEAD_SIZE, heads * PAD)
+    row, col = iota(shape, 0), iota(shape, 1)
+    lane = col & 127
+    part = jnp.where(lane < 64, lane, lane - 16)
+    return one_hot((row == (col >> 7) * HEAD_SIZE + part) & ((lane & 63) < 48))
+
+
+def split_matrix():
+    row, col = iota((RUN, RUN), 0), iota((RUN, RUN), 1)
+    return one_hot(col == jnp.where(row < 128, 2 * row, 2 * row - 255))
+
+
+def merge_matrix():
+    row, col = iota((RUN, RUN), 0), iota((RUN, RUN), 1)
+    return one_hot(col == (row >> 1) + (row & 1) * 128)
+
+
+def rope_tables(run, cb_ref, sb_ref, cj_ref, sj_ref):
+    cb, sb = cb_ref[pl.ds(run, 1), :], sb_ref[pl.ds(run, 1), :]
+    cj, sj = cj_ref[...], sj_ref[...]
+    return cb * cj - sb * sj, sb * cj + cb * sj
+
+
+def rope(u, c, s):
+    return u * c + pltpu.roll(u, 64, 1) * s
+
+
+def rope_back(u, c, s):
+    return u * c - pltpu.roll(u, 64, 1) * s
+
+
+def vmem(*shape_dtype):
+    return pl.BlockSpec(memory_space=pltpu.VMEM)
+
+
+def entry_barrier(targets):
+    bar = pltpu.get_barrier_semaphore()
+    for t in targets:
+        pl.semaphore_signal(bar, inc=1, device_id=t, device_id_type=MESH)
+    pl.semaphore_wait(bar, len(targets))
+
+
+def remote(src, dst, send, recv, target):
+    return pltpu.make_async_remote_copy(
+        src_ref=src, dst_ref=dst, send_sem=send, recv_sem=recv, device_id=target, device_id_type=MESH
+    )
+
+
+def first_kernel(nc, x_ref, dy_h, g_ref, cb_ref, sb_ref, cj_ref, sj_ref, wq_h, wk_h, wv_h, wo_h, wg_h, wu_h, wd_h,
+                 xp_ref, dyp_ref, n1_ref, q_ref, kvp_ref, kvc_ref, wp_ref, gf_ref, wo_f, wg_f, wu_f, wd_f,
+                 dy_v, wq_s, wk_s, wv_s, g_s, wo_v, wg_v, wu_v, wd_v, kv_send,
+                 lsem, ssem, rsem, osem, csem, crem):
+    s = lax.axis_index("shard")
+    c = lax.axis_index("context")
+    dh = g_s.shape[1] // 2
+    own = pl.ds(pl.multiple_of(s * dh, dh), dh)
+    other = {"shard": 1 - s}
+    loads = [
+        pltpu.make_async_copy(wq_h, wq_s.at[own], lsem.at[0]),
+        pltpu.make_async_copy(wk_h, wk_s.at[own], lsem.at[1]),
+        pltpu.make_async_copy(wv_h, wv_s.at[own], lsem.at[2]),
+        pltpu.make_async_copy(g_ref, g_s.at[:, own], lsem.at[3]),
+        pltpu.make_async_copy(wo_h, wo_v, lsem.at[4]),
+        pltpu.make_async_copy(wg_h, wg_v, lsem.at[5]),
+        pltpu.make_async_copy(wu_h, wu_v, lsem.at[6]),
+        pltpu.make_async_copy(wd_h, wd_v, lsem.at[7]),
+        pltpu.make_async_copy(dy_h, dy_v, lsem.at[8]),
+    ]
+    for cp in loads:
+        cp.start()
+    entry_barrier([other] + [{"context": lax.rem(c + i, nc)} for i in range(1, nc)])
+    sends = [
+        remote(wq_s.at[own], wq_s.at[own], ssem.at[0], rsem.at[0], other),
+        remote(wk_s.at[own], wk_s.at[own], ssem.at[1], rsem.at[1], other),
+        remote(wv_s.at[own], wv_s.at[own], ssem.at[2], rsem.at[2], other),
+        remote(g_s.at[:, own], g_s.at[:, own], ssem.at[3], rsem.at[3], other),
+        remote(wo_v, wo_f.at[:, own], ssem.at[4], rsem.at[4], other),
+        remote(wg_v, wg_f.at[own], ssem.at[5], rsem.at[5], other),
+        remote(wu_v, wu_f.at[own], ssem.at[6], rsem.at[6], other),
+        remote(wd_v, wd_f.at[:, own], ssem.at[7], rsem.at[7], other),
+    ]
+    keeps = [
+        pltpu.make_async_copy(wo_v, wo_f.at[:, own], osem.at[0]),
+        pltpu.make_async_copy(wg_v, wg_f.at[own], osem.at[1]),
+        pltpu.make_async_copy(wu_v, wu_f.at[own], osem.at[2]),
+        pltpu.make_async_copy(wd_v, wd_f.at[:, own], osem.at[3]),
+    ]
+    for i in (3, 0, 1, 2, 4, 5, 6, 7):
+        loads[i].wait()
+        sends[i].start()
+        if i >= 4:
+            keeps[i - 4].start()
+    half = x_ref.shape[0] // 2
+    split = split_matrix()
+    for i in range(x_ref.shape[0] // RUN):
+        xb = mm(split, x_ref[pl.ds(i * RUN, RUN), :])
+        xp_ref[pl.ds(i * 128, 128), :] = xb[:128].astype(BF)
+        xp_ref[pl.ds(half + i * 128, 128), :] = xb[128:].astype(BF)
+        if i == 0:
+            sends[3].wait_recv()
+        r = lax.rsqrt(jnp.mean(xb * xb, axis=-1, keepdims=True) + norm_eps)
+        nb = (xb * r * g_s[0:1, :]).astype(BF)
+        n1_ref[pl.ds(i * 128, 128), :] = nb[:128]
+        n1_ref[pl.ds(half + i * 128, 128), :] = nb[128:]
+    gf_ref[...] = g_s[...]
+    hq, hk = wq_s.shape[1] // HEAD_SIZE, wk_s.shape[1] // HEAD_SIZE
+    selq, selk = pad_matrix(hq), pad_matrix(hk)
+    nq, nk = hq * PAD, hk * PAD
+    for i in range(3):
+        sends[i].wait_recv()
+    for i in range(wq_s.shape[0] // RUN):
+        rows = pl.ds(i * RUN, RUN)
+        wp_ref[rows, 0:nq] = mm(wq_s[rows, :], selq).astype(BF)
+        wp_ref[rows, nq : nq + nk] = mm(wk_s[rows, :], selk).astype(BF)
+        wp_ref[rows, nq + nk :] = mm(wv_s[rows, :], selk).astype(BF)
+    selkv = pad_matrix(2 * hk)
+    runs = x_ref.shape[0] // RUN
+    per = runs // 2
+    kv_copies = []
+    for run in range(runs):
+        rows = pl.ds(run * RUN, RUN)
+        y = mm(n1_ref[rows, :], wp_ref[...])
+        ct, st = rope_tables(run, cb_ref, sb_ref, cj_ref, sj_ref)
+        for h in range(hq):
+            q_ref[rows, h * PAD : (h + 1) * PAD] = rope(y[:, h * PAD : (h + 1) * PAD], ct, st).astype(BF)
+        kv = [rope(y[:, nq + h * PAD : nq + (h + 1) * PAD], ct, st).astype(BF) for h in range(hk)]
+        kv = jnp.concatenate(kv + [y[:, nq + nk :].astype(BF)], axis=1)
+        if run < per:
+            kv_send[pl.ds(run * RUN, RUN), :] = mm_nt(kv, selkv).astype(BF)
+            mine = pl.ds(pl.multiple_of((c * per + run) * RUN, RUN), RUN)
+            for i in range(1, nc):
+                cp = remote(kv_send.at[pl.ds(run * RUN, RUN)], kvp_ref.at[mine], csem.at[run, i], crem.at[run, i],
+                            {"context": lax.rem(c + i, nc)})
+                cp.start()
+                kv_copies.append(cp)
+            cp = pltpu.make_async_copy(kv_send.at[pl.ds(run * RUN, RUN)], kvp_ref.at[mine], csem.at[run, 0])
+            cp.start()
+            kv_copies.append(cp)
+        else:
+            kvc_ref[pl.ds((run - per) * RUN, RUN), :] = kv
+    loads[8].wait()
+    for i in range(x_ref.shape[0] // RUN):
+        b = mm(split, dy_v[pl.ds(i * RUN, RUN), :]).astype(BF)
+        dyp_ref[pl.ds(i * 128, 128), :] = b[:128]
+        dyp_ref[pl.ds(half + i * 128, 128), :] = b[128:]
+    for cp in kv_copies:
+        cp.wait()
+    for i in range(4):
+        keeps[i].wait()
+        sends[4 + i].wait_recv()
+    for cp in sends:
+        cp.wait_send()
+
+
+def load_keys(kvp_ref, k_s, v_s, ones):
+    hk = k_s.shape[0]
+    sel = pad_matrix(2 * hk)
+    lane = iota((RUN, PAD), 1)
+
+    def step(i, _):
+        rows = pl.ds(pl.multiple_of(i * RUN, RUN), RUN)
+        kv = mm(kvp_ref[rows, :], sel)
+        for g in range(hk):
+            k_s[g, rows, :] = kv[:, g * PAD : (g + 1) * PAD].astype(BF)
+            v = kv[:, (hk + g) * PAD : (hk + g + 1) * PAD]
+            if ones:
+                v = jnp.where(lane == 48, 1.0, v)
+            v_s[g, rows, :] = v.astype(BF)
+        return 0
+
+    lax.fori_loop(0, kvp_ref.shape[0] // RUN, step, 0)
+
+
+class Line:
+    def __init__(self, n, chunk, jobs, pbuf, rbuf, obuf, sems):
+        self.n, self.chunk, self.per = n, chunk, RUN // 2 // chunk
+        self.count = jobs * self.per
+        self.pbuf, self.rbuf, self.obuf = pbuf, rbuf, obuf
+        self.rs, self.rr, self.bs, self.br = sems
+        self.slots = self.count + 8 * (n - 1) // 3
+
+    def pieces(self, h, i):
+        n, chunk = self.n, self.chunk
+        z = lax.axis_index("tensor")
+        job, off = i // self.per, h * (RUN // 2) + lax.rem(i, self.per) * chunk
+        rows = pl.ds(pl.multiple_of(job * RUN + off, chunk), chunk)
+        there = pl.ds(pl.multiple_of(lax.rem(job, self.rbuf.shape[0] // RUN) * RUN + off, chunk), chunk)
+        place = z if h == 0 else n - 1 - z
+        up, down = jnp.minimum(z + 1, n - 1), jnp.maximum(z - 1, 0)
+        ahead = {"tensor": up if h == 0 else down}
+        back = {"tensor": down if h == 0 else up}
+        fwd = remote(self.pbuf.at[rows], self.rbuf.at[there], self.rs.at[h, i], self.rr.at[h, i], ahead)
+        ret = remote(self.obuf.at[rows], self.obuf.at[rows], self.bs.at[h, i], self.br.at[h, i], back)
+        return rows, there, place, fwd, ret
+
+    def reduce_step(self, h, i):
+        rows, there, place, fwd, ret = self.pieces(h, i)
+        n = self.n
+
+        @pl.when(place == 0)
+        def _():
+            fwd.start()
+
+        @pl.when(place > 0)
+        def _():
+            fwd.wait_recv()
+            total = (self.rbuf[there, :].astype(F32) + self.pbuf[rows, :].astype(F32)).astype(BF)
+
+            @pl.when(place < n - 1)
+            def _():
+                self.pbuf[rows, :] = total
+                fwd.start()
+
+            @pl.when(place == n - 1)
+            def _():
+                self.obuf[rows, :] = total
+                ret.start()
+
+    def spread_step(self, h, i):
+        rows, there, place, fwd, ret = self.pieces(h, i)
+
+        @pl.when(place < self.n - 1)
+        def _():
+            ret.wait_recv()
+
+        @pl.when((place < self.n - 1) & (place > 0))
+        def _():
+            ret.start()
+
+    def serve(self, t):
+        n = self.n
+        z = lax.axis_index("tensor")
+        for h in range(2):
+            place = z if h == 0 else n - 1 - z
+            i = t - (place * 4) // 3
+
+            @pl.when((i >= 0) & (i < self.count))
+            def _():
+                self.reduce_step(h, i)
+
+            j = t - ((2 * (n - 1) - place) * 4) // 3
+
+            @pl.when((j >= 0) & (j < self.count))
+            def _():
+                self.spread_step(h, j)
+
+    def finish(self):
+        def step(i, _):
+            for h in range(2):
+                rows, there, place, fwd, ret = self.pieces(h, i)
+
+                @pl.when(place < self.n - 1)
+                def _():
+                    fwd.wait_send()
+
+                @pl.when(place > 0)
+                def _():
+                    ret.wait_send()
+
+            return 0
+
+        lax.fori_loop(0, self.count, step, 0)
+
+
+def run_items(items, serve):
+    total = max(e for _, e, _ in items)
+
+    def step(k, _):
+        for lo, hi, body in items:
+            pl.when((k >= lo) & (k < hi))(functools.partial(body, k))
+        serve(k)
+        return 0
+
+    lax.fori_loop(0, total, step, 0)
+
+
+class Square:
+    def __init__(self, theirs_src, mine, theirs, r1, r2, res, shard_sems, sems):
+        self.src, self.mine, self.theirs, self.r1, self.r2, self.res = theirs_src, mine, theirs, r1, r2, res
+        self.shard_sems, self.send, self.recv = shard_sems[0], sems[0], sems[1]
+        self.shard_recv = shard_sems[1]
+        self.qr, self.cols = mine.shape[0] // 4, mine.shape[1]
+        c = lax.axis_index("context")
+        self.cy, self.cx = c // 2, lax.rem(c, 2)
+
+    def at(self, y, x, half):
+        w = self.cols // 2
+        return (pl.ds(pl.multiple_of((2 * y + x) * self.qr, self.qr), self.qr), pl.ds(half * w, w))
+
+    def peer(self, half, first):
+        if (half == 0) == first:
+            return {"context": 2 * self.cy + 1 - self.cx}
+        return {"context": 2 * (1 - self.cy) + self.cx}
+
+    def shard_copy(self):
+        return remote(self.src, self.theirs, self.shard_sems, self.shard_recv, {"shard": 1 - lax.axis_index("shard")})
+
+    def outer(self, half):
+        if half == 0:
+            return [(y, 1 - self.cx) for y in range(2)], [(y, self.cx) for y in range(2)]
+        return [(1 - self.cy, x) for x in range(2)], [(self.cy, x) for x in range(2)]
+
+    def p1(self, half, j):
+        return remote(self.mine.at[self.at(*self.outer(half)[0][j], half)], self.r1.at[half, j],
+                      self.send.at[0, half, j], self.recv.at[0, half, j], self.peer(half, True))
+
+    def p2(self, half):
+        q = (1 - self.cy, self.cx) if half == 0 else (self.cy, 1 - self.cx)
+        return remote(self.mine.at[self.at(*q, half)], self.r2.at[half],
+                      self.send.at[1, half, 0], self.recv.at[1, half, 0], self.peer(half, False))
+
+    def p3(self, half):
+        at = self.at(self.cy, self.cx, half)
+        return remote(self.res.at[at], self.res.at[at], self.send.at[1, half, 1], self.recv.at[1, half, 1], self.peer(half, False))
+
+    def p4(self, half, j):
+        at = self.at(*self.outer(half)[1][j], half)
+        return remote(self.res.at[at], self.res.at[at], self.send.at[2, half, j], self.recv.at[2, half, j], self.peer(half, True))
+
+    def e0(self):
+        self.shard_copy().start()
+
+    def e1(self):
+        self.shard_copy().wait_recv()
+        step = self.qr
+
+        def add(i, _):
+            rows = pl.ds(pl.multiple_of(i * step, step), step)
+            self.mine[rows, :] = (self.mine[rows, :].astype(F32) + self.theirs[rows, :].astype(F32)).astype(BF)
+            return 0
+
+        lax.fori_loop(0, self.mine.shape[0] // step, add, 0)
+        for j in range(2):
+            for half in range(2):
+                self.p1(half, j).start()
+
+    def e2(self):
+        for half in range(2):
+            for j in range(2):
+                self.p1(half, j).wait_recv()
+                at = self.at(*self.outer(half)[1][j], half)
+                self.mine[at] = (self.mine[at].astype(F32) + self.r1[half, j].astype(F32)).astype(BF)
+            self.p2(half).start()
+
+    def e3(self):
+        for half in range(2):
+            self.p2(half).wait_recv()
+            at = self.at(self.cy, self.cx, half)
+            self.res[at] = (self.mine[at].astype(F32) + self.r2[half].astype(F32)).astype(BF)
+            self.p3(half).start()
+
+    def e4(self):
+        for half in range(2):
+            self.p3(half).wait_recv()
+            for j in range(2):
+                self.p4(half, j).start()
+
+    def e5(self):
+        for half in range(2):
+            for j in range(2):
+                self.p4(half, j).wait_recv()
+
+    def done(self):
+        self.shard_copy().wait_send()
+        for half in range(2):
+            for j in range(2):
+                self.p1(half, j).wait_send()
+                self.p4(half, j).wait_send()
+            self.p2(half).wait_send()
+            self.p3(half).wait_send()
+
+
+def square_scratch(rows, cols, res=True):
+    q, w = rows // 4, cols // 2
+    out = [pltpu.VMEM((rows, cols), BF), pltpu.VMEM((rows, cols), BF), pltpu.VMEM((2, 2, q, w), BF), pltpu.VMEM((2, q, w), BF)]
+    if res:
+        out.append(pltpu.VMEM((rows, cols), BF))
+    DMA = pltpu.SemaphoreType.DMA
+    return out + [DMA, DMA, DMA((3, 2, 2)), DMA((3, 2, 2))]
+
+
+def line_barrier(n, peers=()):
+    z = lax.axis_index("tensor")
+    bar = pltpu.get_barrier_semaphore()
+    for t in peers:
+        pl.semaphore_signal(bar, inc=1, device_id=t, device_id_type=MESH)
+
+    @pl.when(z > 0)
+    def _():
+        pl.semaphore_signal(bar, inc=1, device_id={"tensor": jnp.maximum(z - 1, 0)}, device_id_type=MESH)
+
+    @pl.when(z < n - 1)
+    def _():
+        pl.semaphore_signal(bar, inc=1, device_id={"tensor": jnp.minimum(z + 1, n - 1)}, device_id_type=MESH)
+
+    pl.semaphore_wait(bar, len(peers) + jnp.minimum(z, 1) + jnp.minimum(n - 1 - z, 1))
+
+
+def mid_kernel(n, chunk, kbase, qlim, q_ref, kvp_ref, kvc_ref, wo_ref, gf_ref, xp_h, dyp_h, wg_h, wu_h, wd_h,
+               o_ref, op_ref, lse_ref, sum_ref, fp_h, gg_h, gu_h, gd_h,
+               k_s, v_s, s_s, pbuf, rbuf, xp_ref, dyp_ref, wg_ref, wu_ref, wd_ref, n2_s, hid_s, dg_s, du_s,
+               st_f, st_g, st_u, st_d, lsem, osem, rs, rr, bs, br):
+    hk = k_s.shape[0]
+    hq = q_ref.shape[1] // PAD
+    rep = hq // hk
+    runs = q_ref.shape[0] // RUN
+    per = runs // 2
+    blocks = kvp_ref.shape[0] // RUN
+    scale = LOG2E / math.sqrt(HEAD_SIZE)
+    pairs = [(xp_h, xp_ref), (wg_h, wg_ref), (wu_h, wu_ref), (dyp_h, dyp_ref), (wd_h, wd_ref)]
+    loads = [pltpu.make_async_copy(a, b, lsem.at[i]) for i, (a, b) in enumerate(pairs)]
+    for cp in loads:
+        cp.start()
+    line_barrier(n)
+    line = Line(n, chunk, 2 * runs, pbuf, rbuf, sum_ref, (rs, rr, bs, br))
+    load_keys(kvp_ref, k_s, v_s, True)
+
+    def head(run, h, own):
+        lane = iota((RUN, PAD), 1)
+        diff = iota((RUN, RUN), 1) - iota((RUN, RUN), 0)
+        rows = pl.ds(pl.multiple_of(run * RUN, RUN), RUN)
+        cols = pl.ds(pl.multiple_of(h * PAD, PAD), PAD)
+        g = h // rep
+        q = q_ref[rows, cols]
+        lim = qlim[run]
+        top = None
+        for b in range(blocks):
+            s = mm_nt(q, k_s[g, pl.ds(b * RUN, RUN), :]) * scale
+            room = lim - kbase[b]
+            if own:
+                s = s + jnp.where(room >= 0, 0.0, NEG)
+            else:
+                s = jnp.where(diff <= room, s, NEG)
+            s_s[:, b * RUN : (b + 1) * RUN] = s
+            top = s if top is None else jnp.maximum(top, s)
+        if own:
+            crow = pl.ds(pl.multiple_of((run - per) * RUN, RUN), RUN)
+            kc = kvc_ref[crow, pl.ds(pl.multiple_of(g * PAD, PAD), PAD)]
+            vc = kvc_ref[crow, pl.ds(pl.multiple_of((hk + g) * PAD, PAD), PAD)]
+            vc = jnp.where(lane == 48, 1.0, vc.astype(F32)).astype(BF)
+            s = jnp.where(diff <= 0, mm_nt(q, kc) * scale, NEG)
+            s_s[:, blocks * RUN :] = s
+            top = jnp.maximum(top, s)
+        m = jnp.max(top, axis=1, keepdims=True)
+        acc = None
+        for b in range(blocks):
+            p = jnp.exp2(s_s[:, b * RUN : (b + 1) * RUN] - m).astype(BF)
+            o = mm(p, v_s[g, pl.ds(b * RUN, RUN), :])
+            acc = o if acc is None else acc + o
+        if own:
+            p = jnp.exp2(s_s[:, blocks * RUN :] - m).astype(BF)
+            acc = acc + mm(p, vc)
+        total = acc[:, 48:49]
+        op_ref[rows, cols] = (acc / total).astype(BF)
+        lse = jnp.broadcast_to(m + jnp.log2(total), (RUN, PAD)).T
+        lse_ref[pl.ds(pl.multiple_of((run * hq + h) * 8, 8), 8), :] = lse[0:8, :]
+
+    def prompt(k):
+        head(k // hq, lax.rem(k, hq), False)
+
+    def cont(k):
+        head(k // hq, lax.rem(k, hq), True)
+
+    def project(k):
+        @pl.when(lax.rem(k, hq) == hq - 1)
+        def _():
+            rows = pl.ds(pl.multiple_of(k // hq * RUN, RUN), RUN)
+            o = mm_nt(op_ref[rows, :], pad_matrix(hq)).astype(BF)
+            o_ref[rows, :] = o
+            pbuf[rows, :] = mm(o, wo_ref[...]).astype(BF)
+
+    ff = wg_ref.shape[1]
+    first = runs * hq
+
+    def ffn(k):
+        i = (k - first) // 4
+        part = lax.rem(k - first, 4)
+        rows = pl.ds(pl.multiple_of(i * RUN, RUN), RUN)
+
+        @pl.when(k == first)
+        def _():
+            for cp in loads:
+                cp.wait()
+
+        @pl.when(part == 0)
+        def _():
+            mid = xp_ref[rows, :].astype(F32) + sum_ref[rows, :].astype(F32)
+            r = lax.rsqrt(jnp.mean(mid * mid, axis=-1, keepdims=True) + norm_eps)
+            n2 = (mid * r * gf_ref[8:9, :]).astype(BF)
+            n2_s[rows, :] = n2
+            s_s[:, 0:ff] = mm(n2, wg_ref[...])
+
+        @pl.when(part == 1)
+        def _():
+            s_s[:, ff : 2 * ff] = mm(n2_s[rows, :], wu_ref[...])
+
+        @pl.when(part == 2)
+        def _():
+            dh = mm_nt(dyp_ref[rows, :], wd_ref[...])
+            gate, up = s_s[:, 0:ff], s_s[:, ff : 2 * ff]
+            sig = jax.nn.sigmoid(gate)
+            silu = gate * sig
+            hid_s[rows, :] = (silu * up).astype(BF)
+            dg_s[rows, :] = (dh * up * sig * (1.0 + gate * (1.0 - sig))).astype(BF)
+            du_s[rows, :] = (dh * silu).astype(BF)
+
+        @pl.when(part == 3)
+        def _():
+            dn = mm_nt(dg_s[rows, :], wg_ref[...]) + mm_nt(du_s[rows, :], wu_ref[...])
+            pbuf[pl.ds(pl.multiple_of((runs + i) * RUN, RUN), RUN), :] = dn.astype(BF)
+
+    second = first + 4 * runs
+
+    def down(k):
+        i = k - second
+        rows = pl.ds(pl.multiple_of(i * RUN, RUN), RUN)
+        cp = pltpu.make_async_copy(st_f, fp_h.at[rows], osem.at[0])
+
+        @pl.when(i > 0)
+        def _():
+            cp.wait()
+
+        st_f[...] = mm(hid_s[rows, :], wd_ref[...]).astype(BF)
+        cp.start()
+
+    third = second + runs
+    d = n2_s.shape[1]
+
+    def grads(k):
+        i = k - third
+        cols = pl.ds(pl.multiple_of(i * RUN, RUN), RUN)
+        cg = pltpu.make_async_copy(st_g, gg_h.at[cols], osem.at[1])
+        cu = pltpu.make_async_copy(st_u, gu_h.at[cols], osem.at[2])
+
+        @pl.when(i > 0)
+        def _():
+            cg.wait()
+            cu.wait()
+
+        nt = n2_s[:, cols].T
+        st_g[...] = mm(nt, dg_s[...]).astype(BF)
+        cg.start()
+        st_u[...] = mm(nt, du_s[...]).astype(BF)
+        cu.start()
+
+    fourth = third + d // RUN
+    wide = d // 2
+
+    def grads_down(k):
+        i = k - fourth
+        cols = pl.ds(pl.multiple_of(i * RUN, RUN), RUN)
+        cp = pltpu.make_async_copy(st_d, gd_h.at[:, cols], osem.at[3])
+
+        @pl.when(i > 0)
+        def _():
+            cp.wait()
+
+        ht = hid_s[:, cols].T
+        for s in range(2):
+            st_d[s] = mm(ht, dyp_ref[:, s * wide : (s + 1) * wide]).astype(BF)
+        cp.start()
+
+    end = fourth + ff // RUN
+    lag = hq - 1
+    items = [(0, per * hq, prompt), (per * hq, first, cont), (0, first, project), (first, second, ffn),
+             (second, third, down), (third, fourth, grads), (fourth, end, grads_down)]
+    if line.slots + lag > end:
+        items.append((end, line.slots + lag, lambda k: None))
+    run_items(items, lambda k: line.serve(k - lag))
+    pltpu.make_async_copy(st_f, fp_h.at[pl.ds(0, RUN)], osem.at[0]).wait()
+    pltpu.make_async_copy(st_g, gg_h.at[pl.ds(0, RUN)], osem.at[1]).wait()
+    pltpu.make_async_copy(st_u, gu_h.at[pl.ds(0, RUN)], osem.at[2]).wait()
+    pltpu.make_async_copy(st_d, gd_h.at[:, pl.ds(0, RUN)], osem.at[3]).wait()
+    line.finish()
+
+
+def back_kernel(n, nc, chunk, kbase, qlim, cb_ref, sb_ref, cj_ref, sj_ref, gf_ref, wo_ref, o_ref, op_ref,
+                lse_ref, q_ref, kvp_ref, kvc_ref, dyp_h, xp_h, sum_h, fp_h, gg_h, gu_h,
+                dm_h, g2_ref, go_ref, dqp_ref, dkvp_ref, dkvc_ref, sf_ref, gg_ref, gu_ref,
+                pbuf, rbuf, ins, st_m, dmb_s, do_s, k_s, v_s, dk_s, dv_s, dq_s, delta_s, lsem, isem, osem, rs, rr, bs, br, *sq):
+    s = lax.axis_index("shard")
+    c = lax.axis_index("context")
+    hk = k_s.shape[0]
+    hq = q_ref.shape[1] // PAD
+    rep = hq // hk
+    rows_here = q_ref.shape[0]
+    runs = rows_here // RUN
+    per = runs // 2
+    blocks = kvp_ref.shape[0] // RUN
+    score = 1.0 / math.sqrt(HEAD_SIZE)
+    scale = LOG2E * score
+    dh = dmb_s.shape[1] // 2
+    mine = pl.ds(pl.multiple_of(s * dh, dh), dh)
+    yours = pl.ds(pl.multiple_of((1 - s) * dh, dh), dh)
+    q1 = Square(gg_h.at[yours], sq[0], sq[1], sq[2], sq[3], gg_ref, (sq[4], sq[5]), (sq[6], sq[7]))
+    q2 = Square(gu_h.at[yours], sq[8], sq[9], sq[10], sq[11], gu_ref, (sq[12], sq[13]), (sq[14], sq[15]))
+    loads = [pltpu.make_async_copy(fp_h, pbuf, lsem.at[0]), pltpu.make_async_copy(gg_h.at[mine], q1.mine, lsem.at[1]),
+             pltpu.make_async_copy(gu_h.at[mine], q2.mine, lsem.at[2])]
+
+    def fetch(i, start):
+        rows = pl.ds(pl.multiple_of(i * RUN, RUN), RUN)
+        late = pl.ds(pl.multiple_of(rows_here + i * RUN, RUN), RUN)
+        slot = lax.rem(i, 2)
+        for j, src in enumerate((xp_h.at[rows], sum_h.at[rows], dyp_h.at[rows], sum_h.at[late])):
+            cp = pltpu.make_async_copy(src, ins.at[slot, j], isem.at[slot, j])
+            if start:
+                cp.start()
+            else:
+                cp.wait()
+
+    fetch(0, True)
+    for cp in loads:
+        cp.start()
+    peers = [{"shard": 1 - s}, {"context": lax.rem(c + 2, 4)}, {"context": c + 1 - 2 * lax.rem(c, 2)}]
+    line_barrier(n, peers)
+    q1.e0()
+    q2.e0()
+    line = Line(n, chunk, runs, pbuf, rbuf, sf_ref, (rs, rr, bs, br))
+    g2_ref[...] = jnp.zeros_like(g2_ref)
+    dk_s[...] = jnp.zeros_like(dk_s)
+    dv_s[...] = jnp.zeros_like(dv_s)
+    loads[0].wait()
+
+    def middle(i):
+        rows = pl.ds(pl.multiple_of(i * RUN, RUN), RUN)
+        slot = lax.rem(i, 2)
+
+        @pl.when(i + 1 < runs)
+        def _():
+            fetch(i + 1, True)
+
+        fetch(i, False)
+        mid = ins[slot, 0].astype(F32) + ins[slot, 1].astype(F32)
+        r = lax.rsqrt(jnp.mean(mid * mid, axis=-1, keepdims=True) + norm_eps)
+        dn = ins[slot, 3].astype(F32)
+        w = gf_ref[8:9, :] * dn
+        inner = jnp.mean(w * mid, axis=-1, keepdims=True)
+        dm = ins[slot, 2].astype(F32) + r * w - mid * (r * r * r) * inner
+        cp = pltpu.make_async_copy(st_m, dm_h.at[rows], osem)
+
+        @pl.when(i > 0)
+        def _():
+            cp.wait()
+
+        st_m[...] = dm
+        cp.start()
+        g2_ref[...] += jnp.sum((dn * mid * r).reshape(RUN // 8, 8, mid.shape[1]), axis=0)
+        dmb = dm.astype(BF)
+        dmb_s[rows, :] = dmb
+        do = mm_nt(dmb, wo_ref[...]).astype(BF)
+        do_s[rows, :] = mm(do, pad_matrix(hq)).astype(BF)
+
+    def out_grad(k):
+        load_keys(kvp_ref, k_s, v_s, False)
+        ot = o_ref[...].T
+        for j in range(2):
+            go_ref[j] = mm(ot, dmb_s[:, j * dh : (j + 1) * dh]).astype(BF)
+
+    width = rep * RUN
+    begin = runs + 1
+
+    def pair(k, own):
+        i, part = (k - begin) // 2, lax.rem(k - begin, 2)
+        run, g = i // hk, lax.rem(i, hk)
+        rows = pl.ds(pl.multiple_of(run * RUN, RUN), RUN)
+        diff = iota((RUN, width), 0) - (iota((RUN, width), 1) & (RUN - 1))
+
+        def stack(ref):
+            parts = [ref[rows, pl.ds(pl.multiple_of((g * rep + j) * PAD, PAD), PAD)] for j in range(rep)]
+            return jnp.concatenate(parts, axis=0)
+
+        q, do = stack(q_ref), stack(do_s)
+
+        @pl.when(part == 0)
+        def _():
+            op = stack(op_ref)
+            delta_s[0:1, :] = jnp.sum((do.astype(F32) * op.astype(F32)).T, axis=0, keepdims=True)
+            dq_s[...] = jnp.zeros_like(dq_s)
+
+        delta = delta_s[0:1, :]
+        lse = jnp.concatenate(
+            [lse_ref[pl.ds(pl.multiple_of((run * hq + g * rep + j) * 8, 8), 1), :] for j in range(rep)], axis=1
+        )
+        lim = qlim[run]
+
+        def tile(k, v, hide):
+            p = jnp.exp2(hide(mm_nt(k, q) * scale - lse))
+            ds = (p * (mm_nt(v, do) - delta)).astype(BF)
+            return mm(ds, q), mm(p.astype(BF), do), mm_tn(ds, k)
+
+        dq = dq_s[...]
+        for bb in range(blocks // 2):
+            b = part * (blocks // 2) + bb
+            at = pl.ds(pl.multiple_of(b * RUN, RUN), RUN)
+            room = lim - kbase[b]
+            if own:
+                hide = lambda t: t + jnp.where(room >= 0, 0.0, NEG)
+            else:
+                hide = lambda t: jnp.where(diff <= room, t, NEG)
+            dk, dv, dd = tile(k_s[g, at, :], v_s[g, at, :], hide)
+            dk_s[g, at, :] += dk
+            dv_s[g, at, :] += dv
+            dq = dq + dd
+        dq_s[...] = dq
+
+        @pl.when(part == 1)
+        def _():
+            total = dq_s[...]
+            ct, st = rope_tables(run, cb_ref, sb_ref, cj_ref, sj_ref)
+            if own:
+                crow = pl.ds(pl.multiple_of((run - per) * RUN, RUN), RUN)
+                kcol = pl.ds(pl.multiple_of(g * PAD, PAD), PAD)
+                vcol = pl.ds(pl.multiple_of((hk + g) * PAD, PAD), PAD)
+                dk, dv, dd = tile(kvc_ref[crow, kcol], kvc_ref[crow, vcol], lambda t: jnp.where(diff <= 0, t, NEG))
+                total = total + dd
+                dkvc_ref[crow, kcol] = rope_back(dk * score, ct, st).astype(BF)
+                dkvc_ref[crow, vcol] = dv.astype(BF)
+            for j in range(rep):
+                dqp_ref[rows, pl.ds(pl.multiple_of((g * rep + j) * PAD, PAD), PAD)] = rope_back(
+                    total[j * RUN : (j + 1) * RUN] * score, ct, st
+                ).astype(BF)
+
+    middle_end = begin + 2 * per * hk
+    end = begin + 2 * runs * hk
+
+    def pack(k):
+        def one(i, _):
+            rows = pl.ds(pl.multiple_of(i * RUN, RUN), RUN)
+            parts = [(dk_s[g, rows, :] * score).astype(BF) for g in range(hk)]
+            parts += [dv_s[g, rows, :].astype(BF) for g in range(hk)]
+            dkvp_ref[rows, :] = mm_nt(jnp.concatenate(parts, axis=1), pad_matrix(2 * hk)).astype(BF)
+            return 0
+
+        lax.fori_loop(0, blocks, one, 0)
+
+    def when(*events):
+        def body(k):
+            for e in events:
+                e()
+
+        return body
+
+    def first_wait():
+        loads[1].wait()
+        loads[2].wait()
+
+    items = [(0, runs, middle), (runs, begin, out_grad), (begin, middle_end, lambda k: pair(k, False)),
+             (middle_end, end, lambda k: pair(k, True)), (end, end + 1, pack)]
+    order = [(2, first_wait), (3, q1.e1), (5, q2.e1), (7, q1.e2), (10, q2.e2), (11, q1.e3), (13, q1.e4), (14, q2.e3), (16, q2.e4), (18, q1.e5), (20, q2.e5)]
+    items += [(k, k + 1, when(e)) for k, e in order]
+    if line.slots > end + 1:
+        items.append((end + 1, line.slots, lambda k: None))
+    run_items(items, line.serve)
+    pltpu.make_async_copy(st_m, dm_h.at[pl.ds(0, RUN)], osem).wait()
+    line.finish()
+    q1.done()
+    q2.done()
+
+
+def last_kernel(n, nc, chunk, cb_ref, sb_ref, cj_ref, sj_ref, dkvp_ref, dkvc_ref, dqp_ref, n1_h, wp_ref, gf_ref, g2_ref,
+                xp_h, sum_h, sf_h, dm_h, gd_h, go_h,
+                out_ref, tg_ref, gg_ref, gd_ref, go_ref, gw_ref,
+                n1_ref, xp_ref, ins, st_o, st_t, dm_ref, recv, dkv_s, gw_s, pbuf, rbuf, obuf, gpart, grecv,
+                lsem, isem, osem, ssem, rsem, gs, gr, rs, rr, bs, br, *sq):
+    s = lax.axis_index("shard")
+    c = lax.axis_index("context")
+    rows_here = dqp_ref.shape[0]
+    half = rows_here // 2
+    runs = rows_here // RUN
+    per = runs // 2
+    nq, nkv = dqp_ref.shape[1], dkvc_ref.shape[1]
+    hk, hq = nkv // PAD // 2, nq // PAD
+    d = n1_ref.shape[1]
+    dh = d // 2
+    mine = pl.ds(pl.multiple_of(s * dh, dh), dh)
+    yours = pl.ds(pl.multiple_of((1 - s) * dh, dh), dh)
+    q1 = Square(gd_h.at[1 - s], sq[0], sq[1], sq[2], sq[3], gd_ref, (sq[4], sq[5]), (sq[6], sq[7]))
+    q2 = Square(go_h.at[1 - s], sq[8], sq[9], sq[10], sq[11], go_ref, (sq[12], sq[13]), (sq[14], sq[15]))
+    q3 = Square(gw_s.at[yours], gw_s.at[mine], sq[16], sq[17], sq[18], gw_ref, (sq[19], sq[20]), (sq[21], sq[22]))
+    pairs = [(n1_h, n1_ref), (gd_h.at[s], q1.mine), (go_h.at[s], q2.mine), (xp_h, xp_ref), (dm_h, dm_ref)]
+    loads = [pltpu.make_async_copy(a, b, lsem.at[i]) for i, (a, b) in enumerate(pairs)]
+    for cp in loads:
+        cp.start()
+    peers = [{"shard": lax.rem(s + i // nc, 2), "context": lax.rem(c + lax.rem(i, nc), nc)} for i in range(1, 2 * nc)]
+    line_barrier(n, peers)
+    copies = []
+    for i in range(1, nc):
+        to = lax.rem(c + i, nc)
+        cp = remote(dkvp_ref.at[pl.ds(pl.multiple_of(to * half, half), half)], recv.at[i - 1], ssem.at[i - 1], rsem.at[i - 1],
+                    {"context": to})
+        cp.start()
+        copies.append(cp)
+    q1.e0()
+    q2.e0()
+    line = Line(n, chunk, runs, pbuf, rbuf, obuf, (rs, rr, bs, br))
+
+    def normed(run, job):
+        rows = pl.ds(run * RUN, RUN)
+        dn = mm_nt(dqp_ref[rows, :], wp_ref[:, 0:nq]) + mm_nt(dkv_s[rows, :], wp_ref[:, nq:])
+        pbuf[pl.ds(job * RUN, RUN), :] = dn.astype(BF)
+
+    wide_q = hq * HEAD_SIZE
+
+    def start(k):
+        dkv_s[pl.ds(half, half), :] = dkvc_ref[...]
+        normed(per, 0)
+
+    def more(k):
+        for i in range(1, per):
+            normed(per + i, i)
+
+    def grads_q(k):
+        i = k - 2
+
+        @pl.when(i == 0)
+        def _():
+            loads[0].wait()
+
+        dq_u = mm_nt(dqp_ref[...], pad_matrix(hq)).astype(BF)
+        for j in range(2):
+            cols = pl.ds(pl.multiple_of((2 * i + j) * RUN, RUN), RUN)
+            gw_s[cols, 0:wide_q] = mm(n1_ref[:, cols].T, dq_u).astype(BF)
+
+    nq_items = d // RUN // 2
+
+    def keys(k):
+        for cp in copies:
+            cp.wait_recv()
+        selkv = pad_matrix(2 * hk)
+        for run in range(per):
+            rows = pl.ds(run * RUN, RUN)
+            at = pl.ds(pl.multiple_of(c * half + run * RUN, RUN), RUN)
+            total = mm(dkvp_ref[at, :], selkv)
+            for i in range(nc - 1):
+                total = total + mm(recv[i, rows, :], selkv)
+            ct, st = rope_tables(run, cb_ref, sb_ref, cj_ref, sj_ref)
+            for g in range(hk):
+                dkv_s[rows, g * PAD : (g + 1) * PAD] = rope_back(total[:, g * PAD : (g + 1) * PAD], ct, st).astype(BF)
+            dkv_s[rows, hk * PAD :] = total[:, hk * PAD :].astype(BF)
+            normed(run, per + run)
+
+    def grads_kv(k):
+        dkv_u = mm_nt(dkv_s[...], pad_matrix(2 * hk)).astype(BF)
+
+        def one(i, _):
+            cols = pl.ds(pl.multiple_of(i * RUN, RUN), RUN)
+            gw_s[cols, wide_q:] = mm(n1_ref[:, cols].T, dkv_u).astype(BF)
+            return 0
+
+        lax.fori_loop(0, d // RUN, one, 0)
+        q3.e0()
+
+    def take(ref, lo, hi):
+        return jnp.concatenate([ref[pl.ds(pl.multiple_of(lo, 128), 128), :], ref[pl.ds(pl.multiple_of(hi, 128), 128), :]], axis=0).astype(F32)
+
+    def fetch(i, start):
+        slot = lax.rem(i, 2)
+        for j, src in enumerate((sum_h, sf_h)):
+            for m in range(2):
+                at = pl.ds(pl.multiple_of(m * half + i * 128, 128), 128)
+                cp = pltpu.make_async_copy(src.at[at], ins.at[slot, j, pl.ds(m * 128, 128)], isem.at[slot, j, m])
+                if start:
+                    cp.start()
+                else:
+                    cp.wait()
+
+    fetch(0, True)
+    ak = 2 + nq_items
+    out_at = ak + 2
+
+    def output(k):
+        i = k - out_at
+
+        @pl.when(i == 0)
+        def _():
+            for cp in loads[3:]:
+                cp.wait()
+            gpart[0:8, :] = jnp.zeros((8, d), F32)
+            gpart[8:16, :] = g2_ref[...]
+
+        @pl.when(i + 1 < runs)
+        def _():
+            fetch(i + 1, True)
+
+        fetch(i, False)
+        slot = lax.rem(i, 2)
+        lo, hi = i * 128, half + i * 128
+        mid = take(xp_ref, lo, hi) + ins[slot, 0].astype(F32)
+        rows = pl.ds(pl.multiple_of(i * RUN, RUN), RUN)
+        cp = pltpu.make_async_copy(st_o, out_ref.at[rows], osem.at[0])
+
+        @pl.when(i > 0)
+        def _():
+            cp.wait()
+
+        st_o[...] = mm(merge_matrix(), (mid + ins[slot, 1].astype(F32)).astype(BF)).astype(BF)
+        cp.start()
+
+    def finals(i):
+        lo, hi = i * 128, half + i * 128
+        x = take(xp_ref, lo, hi)
+        dn = take(obuf, half + lo, lo)
+        r = lax.rsqrt(jnp.mean(x * x, axis=-1, keepdims=True) + norm_eps)
+        w = gf_ref[0:1, :] * dn
+        inner = jnp.mean(w * x, axis=-1, keepdims=True)
+        tg = take(dm_ref, lo, hi) + (r * w - x * (r * r * r) * inner)
+        rows = pl.ds(pl.multiple_of(i * RUN, RUN), RUN)
+        cp = pltpu.make_async_copy(st_t, tg_ref.at[rows], osem.at[1])
+
+        @pl.when(i > 0)
+        def _():
+            cp.wait()
+
+        st_t[...] = mm(merge_matrix(), tg.astype(BF)).astype(BF)
+        cp.start()
+        gpart[0:8, :] += jnp.sum((dn * x * r).reshape(RUN // 8, 8, d), axis=0)
+
+    ready = (per + 1) * line.per + 8 * (n - 1) // 3
+
+    def tail(k):
+        j = (k - ready) // line.per
+        part = lax.rem(k - ready, line.per)
+
+        @pl.when(part < 2)
+        def _():
+            finals(2 * j + part)
+
+    def event(e):
+        return lambda k: e()
+
+    def begin_squares():
+        loads[1].wait()
+        loads[2].wait()
+        q1.e1()
+
+    last = ready + (per - 1) * line.per
+    items = [(0, 1, start), (1, 2, more), (2, ak, grads_q), (ak, ak + 1, keys), (ak + 1, ak + 2, grads_kv),
+             (out_at, out_at + runs, output), (ready, last, tail), (last, line.slots, lambda k: None)]
+    order = [(3, begin_squares), (4, q2.e1), (6, q1.e2), (7, q2.e2), (9, q1.e3), (10, q2.e3), (10, q3.e1), (11, q1.e4), (12, q2.e4), (13, q3.e2),
+             (15, q3.e3), (17, q3.e4), (18, q1.e5), (18, q2.e5), (20, q3.e5)]
+    items += [(k, k + 1, event(e)) for k, e in order]
+    run_items(items, line.serve)
+    for i in range(2):
+        finals(jnp.int32(2 * (per - 1) + i))
+    me = s * nc + c
+    sums = jnp.concatenate(
+        [jnp.broadcast_to(jnp.sum(gpart[k * 8 : (k + 1) * 8, :], axis=0, keepdims=True), (8, d)) for k in range(2)], axis=0
+    )
+    grecv[me] = sums
+    gcopies = []
+    for i, t in enumerate(peers):
+        cp = remote(grecv.at[me], grecv.at[me], gs.at[i], gr.at[i], t)
+        cp.start()
+        gcopies.append(cp)
+    line.finish()
+    for q in (q1, q2, q3):
+        q.done()
+    for cp in copies:
+        cp.wait_send()
+    for cp in gcopies:
+        cp.wait()
+    pltpu.make_async_copy(st_o, out_ref.at[pl.ds(0, RUN)], osem.at[0]).wait()
+    pltpu.make_async_copy(st_t, tg_ref.at[pl.ds(0, RUN)], osem.at[1]).wait()
+    total = grecv[0]
+    for i in range(1, 2 * nc):
+        total = total + grecv[i]
+    gg_ref[...] = total
+
+
+def fast(
+    tokens, w_query, key_weight, value_weight, w_out, w_gate, w_up, w_down, gain_attn, gain_ffn, segments, positions, cotangent, n, nc
+):
+    _, rows, d = tokens.shape
+    half = rows // 2
+    runs = rows // RUN
+    per = runs // 2
+    prompt = segments.shape[1] // 2
+    blocks = prompt // RUN
+    dq, dk = w_query.shape[1], key_weight.shape[1]
+    hq, hk = dq // HEAD_SIZE, dk // HEAD_SIZE
+    nq, nk = hq * PAD, hk * PAD
+    ff = w_gate.shape[1]
+    dh = d // 2
+    c = lax.axis_index("context")
+    x = tokens.reshape(rows, d)
+    dy = cotangent.reshape(rows, d)
+    kbase = positions[0, 0 :: 2 * RUN]
+    seg_here = lax.dynamic_slice_in_dim(segments[0], c * rows, rows, 0)
+    pos_here = lax.dynamic_slice_in_dim(positions[0], c * rows, rows, 0)
+    qbase = jnp.concatenate([pos_here[0 :: 2 * RUN], pos_here[1 :: 2 * RUN]])
+    qlim = jnp.concatenate([pos_here[0 :: 2 * RUN], seg_here[1 :: 2 * RUN] * CLEN - 1])
+    freq = np.exp(np.arange(HEAD_SIZE // 2, dtype=np.float32) * np.float32(-2.0 * math.log(rope_base) / HEAD_SIZE)).astype(np.float32)
+    lanes = np.zeros((PAD,), np.float32)
+    lanes[0:48] = freq
+    lanes[64:112] = freq
+    sign = np.where(np.arange(PAD) < 64, -1.0, 1.0).astype(np.float32)
+    inner = np.arange(RUN, dtype=np.float64)[:, None] * lanes[None, :].astype(np.float64)
+    cj = jnp.asarray(np.cos(inner).astype(np.float32))
+    sj = jnp.asarray((np.sin(inner) * sign).astype(np.float32))
+    angle = qbase.astype(F32)[:, None] * jnp.asarray(lanes)[None, :]
+    cb = jnp.cos(angle)
+    sb = jnp.sin(angle) * jnp.asarray(sign)[None, :]
+    gains = jnp.concatenate([jnp.broadcast_to(g.astype(F32)[None, :], (8, dh)) for g in (gain_attn, gain_ffn)], axis=0)
+
+    V = pl.BlockSpec(memory_space=pltpu.VMEM)
+    S = pl.BlockSpec(memory_space=pltpu.SMEM)
+    A = pl.BlockSpec(memory_space=pl.ANY)
+    sds = jax.ShapeDtypeStruct
+    DMA = pltpu.SemaphoreType.DMA
+
+    def call(kernel, ins, outs, scratch, collective=None, flops=0):
+        params = dict(vmem_limit_bytes=VLIM - 64 * 1024)
+        if collective is not None:
+            params.update(collective_id=collective, has_side_effects=True)
+        args = [a for a, _ in ins]
+        return pl.pallas_call(
+            kernel,
+            out_shape=[o for o, _ in outs],
+            in_specs=[sp for _, sp in ins],
+            out_specs=[sp for _, sp in outs],
+            scratch_shapes=scratch,
+            compiler_params=pltpu.CompilerParams(**params),
+            cost_estimate=pl.CostEstimate(flops=flops, bytes_accessed=0, transcendentals=0),
+        )(*args)
+
+    rope_in = [(cb, V), (sb, V), (cj, V), (sj, V)]
+    xp, dyp, n1, q, kvp, kvc, wp, gf, wo, wg, wu, wd = call(
+        functools.partial(first_kernel, nc),
+        [(x, V), (dy, A), (gains, A)] + rope_in + [(w_query, A), (key_weight, A), (value_weight, A), (w_out, A), (w_gate, A), (w_up, A), (w_down, A)],
+        [
+            (sds((rows, d), BF), V), (sds((rows, d), BF), V), (sds((rows, d), BF), V), (sds((rows, nq), BF), V),
+            (sds((prompt, 2 * dk), BF), A), (sds((half, 2 * nk), BF), V), (sds((d, nq + 2 * nk), BF), V), (sds((16, d), F32), V),
+            (sds((dq, d), BF), A), (sds((d, ff), BF), A), (sds((d, ff), BF), A), (sds((ff, d), BF), A),
+        ],
+        [
+            pltpu.VMEM((rows, d), BF), pltpu.VMEM((d, dq), BF), pltpu.VMEM((d, dk), BF), pltpu.VMEM((d, dk), BF), pltpu.VMEM((16, d), F32),
+            pltpu.VMEM((dq, dh), BF), pltpu.VMEM((dh, ff), BF), pltpu.VMEM((dh, ff), BF), pltpu.VMEM((ff, dh), BF),
+            pltpu.VMEM((half, 2 * dk), BF),
+            DMA((9,)), DMA((8,)), DMA((8,)), DMA((4,)), DMA((per, nc)), DMA((per, nc)),
+        ],
+        collective=0, flops=60 * 10**9,
+    )
+
+    chunk = 32
+    per_half = RUN // 2 // chunk
+
+    def sums(jobs):
+        return [DMA((2, jobs * per_half))] * 4
+
+    o, op, lse, sum12, fp, gg, gu, gd = call(
+        functools.partial(mid_kernel, n, chunk),
+        [(kbase, S), (qlim, S), (q, V), (kvp, V), (kvc, V), (wo, V), (gf, V), (xp, A), (dyp, A), (wg, A), (wu, A), (wd, A)],
+        [(sds((rows, dq), BF), V), (sds((rows, nq), BF), V), (sds((runs * hq * 8, RUN), F32), V), (sds((2 * rows, d), BF), V),
+         (sds((rows, d), BF), A), (sds((d, ff), BF), A), (sds((d, ff), BF), A), (sds((2, ff, dh), BF), A)],
+        [pltpu.VMEM((hk, prompt, PAD), BF), pltpu.VMEM((hk, prompt, PAD), BF), pltpu.VMEM((RUN, prompt + RUN), F32),
+         pltpu.VMEM((2 * rows, d), BF), pltpu.VMEM((rows, d), BF), pltpu.VMEM((rows, d), BF), pltpu.VMEM((rows, d), BF),
+         pltpu.VMEM((d, ff), BF), pltpu.VMEM((d, ff), BF), pltpu.VMEM((ff, d), BF),
+         pltpu.VMEM((rows, d), BF), pltpu.VMEM((rows, ff), BF), pltpu.VMEM((rows, ff), BF), pltpu.VMEM((rows, ff), BF),
+         pltpu.VMEM((RUN, d), BF), pltpu.VMEM((RUN, ff), BF), pltpu.VMEM((RUN, ff), BF), pltpu.VMEM((2, RUN, dh), BF),
+         DMA((5,)), DMA((4,))] + sums(2 * runs),
+        collective=1, flops=160 * 10**9,
+    )
+    dm, g2, go, dqp, dkvp, dkvc, sf, gg, gu = call(
+        functools.partial(back_kernel, n, nc, chunk),
+        [(kbase, S), (qlim, S)] + rope_in
+        + [(gf, V), (wo, V), (o, V), (op, V), (lse, V), (q, V), (kvp, V), (kvc, V), (dyp, A), (xp, A), (sum12, A), (fp, A), (gg, A), (gu, A)],
+        [(sds((rows, d), F32), A), (sds((8, d), F32), V), (sds((2, dq, dh), BF), V), (sds((rows, nq), BF), V),
+         (sds((prompt, 2 * dk), BF), V), (sds((half, 2 * nk), BF), V), (sds((rows, d), BF), V), (sds((dh, ff), BF), V), (sds((dh, ff), BF), V)],
+        [pltpu.VMEM((rows, d), BF), pltpu.VMEM((rows, d), BF), pltpu.VMEM((2, 4, RUN, d), BF), pltpu.VMEM((RUN, d), F32),
+         pltpu.VMEM((rows, d), BF), pltpu.VMEM((rows, nq), BF), pltpu.VMEM((hk, prompt, PAD), BF), pltpu.VMEM((hk, prompt, PAD), BF),
+         pltpu.VMEM((hk, prompt, PAD), F32), pltpu.VMEM((hk, prompt, PAD), F32), pltpu.VMEM((hq // hk * RUN, PAD), F32),
+         pltpu.VMEM((8, hq // hk * RUN), F32), DMA((3,)), DMA((2, 4)), DMA] + sums(runs)
+        + square_scratch(dh, ff, False) + square_scratch(dh, ff, False),
+        collective=2, flops=100 * 10**9,
+    )
+    out, tg, gains_grad, gd, go, gw = call(
+        functools.partial(last_kernel, n, nc, chunk),
+        rope_in + [(dkvp, V), (dkvc, V), (dqp, V), (n1, A), (wp, V), (gf, V), (g2, V), (xp, A), (sum12, A), (sf, A), (dm, A), (gd, A), (go, A)],
+        [(sds((rows, d), BF), A), (sds((rows, d), BF), A), (sds((16, d), F32), V), (sds((ff, dh), BF), V), (sds((dq, dh), BF), V),
+         (sds((dh, dq + 2 * dk), BF), V)],
+        [pltpu.VMEM((rows, d), BF), pltpu.VMEM((rows, d), BF), pltpu.VMEM((2, 2, RUN, d), BF), pltpu.VMEM((RUN, d), BF), pltpu.VMEM((RUN, d), BF),
+         pltpu.VMEM((rows, d), F32),
+         pltpu.VMEM((nc - 1, half, 2 * dk), BF), pltpu.VMEM((rows, 2 * nk), BF), pltpu.VMEM((d, dq + 2 * dk), BF),
+         pltpu.VMEM((rows, d), BF), pltpu.VMEM((rows, d), BF), pltpu.VMEM((rows, d), BF),
+         pltpu.VMEM((16, d), F32), pltpu.VMEM((2 * nc, 16, d), F32), DMA((5,)), DMA((2, 2, 2)), DMA((2,)), DMA((nc - 1,)), DMA((nc - 1,)),
+         DMA((2 * nc - 1,)), DMA((2 * nc - 1,))] + sums(runs)
+        + square_scratch(ff, dh, False) + square_scratch(dq, dh, False) + square_scratch(dh, dq + 2 * dk, False)[1:],
+        collective=3, flops=160 * 10**9,
+    )
+    s = lax.axis_index("shard")
+    g1o = lax.dynamic_slice_in_dim(gains_grad[0], s * dh, dh, 0)
+    g2o = lax.dynamic_slice_in_dim(gains_grad[8], s * dh, dh, 0)
+    return (
+        out[None], tg[None],
+        gw[:, :dq].astype(F32), gw[:, dq : dq + dk].astype(F32), gw[:, dq + dk :].astype(F32),
+        go.astype(F32), gg.astype(F32), gu.astype(F32), gd.astype(F32), g1o, g2o,
+    )
+
+
+def body(mesh, *args):
+    tokens, w_query, segments = args[0], args[1], args[10]
+    n, nc = mesh.shape["tensor"], mesh.shape["context"]
+    rows = tokens.shape[1]
+    if (tokens.shape[0] == 1 and rows % (4 * CLEN) == 0 and n > 1 and nc == 4 and mesh.shape["shard"] == 2
+            and segments.shape[1] == rows * nc):
+        return fast(*args, n, nc)
+    return general(*args)
+
+
 def solution(mesh):
     in_specs = (
         P("shard", "context", None),
@@ -390,4 +1534,4 @@
         P("shard"),
         P("shard"),
     )
-    return jax.shard_map(body, mesh=mesh, in_specs=in_specs, out_specs=out_specs, check_vma=False)
+    return jax.shard_map(functools.partial(body, mesh), mesh=mesh, in_specs=in_specs, out_specs=out_specs, check_vma=False)

time: 1620 us -> 473 us (0.29)
  waiting for transfers between devices: 1060 us -> 0 us
  Pallas kernels: 0 us -> 433 us
  matrix products: 261 us -> 0 us
  other arithmetic: 156 us -> 14.5 us
  blocking collectives: 74.8 us -> 0 us
  local copies, waits for them, and re-layouts: 36.4 us -> 17.4 us
    psum x4 -> x0, waiting for transfers between devices: 734 us -> none  [the longest x1 219 us: body(): lax.psum(jnp.dot(attended_low, w_out, preferred_element_type=jnp.float32)...]
    pallas_call x0 -> x4, Pallas kernels: none -> 433 us  [call(): pl.pallas_call(kernel, out_shape=[o for o, _ in outs], in_specs=[sp for _...]
    dot_general x27 -> x0, matrix products: 261 us -> none  [the longest x1 45.7 us: attend_back(): jnp.einsum('bhgd,khd->hgbk', grad_grouped, value_head_rows, preferred_ele...]
    reduce_scatter x8 -> x0, waiting for transfers between devices: 203 us -> none  [the longest x1 69.4 us: body(): lax.psum_scatter(grad_keyval, 'context', scatter_dimension=1, tiled=True)]
    all_gather x9 -> x0, waiting for transfers between devices: 123 us -> none  [the longest x1 29.1 us: body(): lax.all_gather(summed[5].astype(jnp.bfloat16), 'context', axis=0, tiled=T...]
    convert_element_type x19 -> x6, other arithmetic: 77.3 us -> 11.9 us  [the longest x1 3.3 us: fast(): gd.astype(F32)]
    all_gather x8 -> x0, blocking collectives: 41.6 us -> none  [the longest x1 8.24 us: body(): lax.all_gather(summed[3].astype(jnp.bfloat16), 'context', axis=0, tiled=T...]
    reduce_sum x5 -> x0, other arithmetic: 38.2 us -> none  [the longest x1 21.2 us: attend_group(): totals = jnp.sum(exponent, axis=-1, keepdims=True)]
  transfers between devices with their start and end apart: 21 -> 0, of which waited for: 16 -> 0; matrix products, arithmetic and copies ran while one was open for 25% -> 0% of each run, Pallas kernels for 0% -> 0%
where the time goes in v2:
time: 473 us; the launch traced here: 466 us
  Pallas kernels  433 us (92%)
  local copies, waits for them, and re-layouts  17.4 us (4%)
  other arithmetic  14.5 us (3%)
    pallas_call x4, Pallas kernels, call(): pl.pallas_call(kernel, out_shape=[o for o, _ in outs], in_specs=[sp for _...  433 us
    unnamed x16, local copies, waits for them, and re-layouts  11.6 us

profile of v2, /device:TPU:1, one launch (start us, length us, event | category | flops | bytes accessed | tf_op | source)
XLA Modules:
  0.0 465.8 jit_solution(11997158183150512374)
XLA Ops:
  0.6 1.3 slice.30
  2.0 0.7 constant_dynamic-slice_fusion
  3.5 1.4 fusion
  4.9 0.7 broadcast_in_dim.8
  5.6 0.7 broadcast_in_dim.9
  6.3 0.6 pad_maximum_fusion.g_ref
  6.9 1.9 copy.28.wk_h
  8.8 1.9 copy.29.wv_h
  10.7 34.9 %shard_map.248 = (bf16[1024,1536]{1,0:T(8,128)(2,1)}, bf16[1024,1536]{1,0:T(8,128)(2,1)}, bf16[1024,1536]{1,0:T(8,128)(2,1)}, bf16[1024,512]{1,0:T(8,128)(2,1)},...) custom-call(bf16[1024,1536]{1,0:T(8,128)(2,1)} %bitcast.12, ...), custom_call_target="tpu_custom_call" | custom-call | flops 60000002048 | tf_op jit(solution)/shard_map/pallas_call | solution.py:1414
  45.5 166.0 %shard_map.249 = (bf16[1024,384]{1,0:T(8,128)(2,1)}, bf16[1024,512]{1,0:T(8,128)(2,1)}, f32[128,256]{1,0:T(8,128)}, bf16[2048,1536]{1,0:T(8,128)(2,1)}, bf16[102...) custom-call(s32[8]{0:T(128)} %bitcast.14, ...), custom_call_target="tpu_custom_call" | custom-call | flops 160000000000 | tf_op jit(solution)/shard_map/pallas_call | solution.py:1414
  211.6 109.9 %shard_map.250 = (f32[1024,1536]{1,0:T(8,128)}, f32[8,1536]{1,0:T(8,128)}, bf16[2,384,768]{2,1,0:T(8,128)(2,1)}, bf16[1024,512]{1,0:T(8,128)(2,1)}, bf16[2048,38...) custom-call(s32[8]{0:T(128)} %bitcast.15, ...), custom_call_target="tpu_custom_call" | custom-call | flops 99999997952 | tf_op jit(solution)/shard_map/pallas_call | solution.py:1414
  321.5 121.9 %shard_map.251 = (bf16[1024,1536]{1,0:T(8,128)(2,1)}, bf16[1024,1536]{1,0:T(8,128)(2,1)}, f32[16,1536]{1,0:T(8,128)}, bf16[1024,768]{1,0:T(8,128)(2,1)}, bf16[38...) custom-call(f32[4,128]{1,0:T(4,128)} %get-tuple-element.97.cb_ref, f32[4,128]{1,0:T(4,128)} %get-tuple-element.96.sb_ref, ...), custom_call_target="tpu_custom_call" | custom-call | flops 160000000000 | tf_op jit(solution)/shard_map/pallas_call | solution.py:1414
  443.5 0.9 fusion.1
  445.6 2.2 convert_element_type.40
  447.7 2.2 slice_convert_fusion
  450.1 1.1 copy.31
  451.2 1.1 copy.30
  452.2 3.3 convert_element_type.43
  455.6 2.1 convert_element_type.41
  457.6 2.1 convert_element_type.42
  459.7 1.0 copy-done.1
  460.6 1.7 copy.34
  462.3 1.4 copy-done
  463.7 1.7 copy.35
  (16 shorter events, 2.3 us)
Async XLA Ops:
  443.4 6.5 %copy-start.2 = (bf16[768,768]{1,0:T(8,128)(2,1)S(1)}, bf16[768,768]{1,0:T(8,128)(2,1)}, u32[]{:S(2)}) copy-start(bf16[768,768]{1,0:T(8,128)(2,1)} %get-tuple-element.75) | copy-start | bytes 3538948
  451.2 4.4 copy-start.4
  455.6 2.1 copy-start.3
  457.6 3.0 copy-start.1
  460.6 3.0 copy-start
